TPU v7x, 128 devices: a whole 4x4x4 slice. The times are simulated.
128 devices in a mesh: pool: 2 (over core), grp: 4 (over y), rep: 16 (over x, z).
Axes of the slice: x: 4, y: 4, z: 4, core: 2. Of those that a mesh axis runs over, the one named last changes fastest.
Arguments:
- queries: bfloat16 [512, 8192], P('pool', 'grp'), may hold values from -64 to 64
- keys: bfloat16 [16384, 512], P('rep', 'grp'), may hold values from -7 to 7
- values: bfloat16 [16384, 512], P('rep', 'grp'), may hold values from -6 to 6
- hidden_in: bfloat16 [512, 4096], P(('pool', 'grp', 'rep')), may hold values from -4 to 4
- o_weight: bfloat16 [8192, 4096], P('grp', 'rep'), may hold values from -0.125 to 0.125
- norm_gain: bfloat16 [4096], replicated, may hold values from 0.5 to 1.5
- routes: int32 [512, 8], P(('pool', 'grp', 'rep')), may hold values from 0 to 63, as said below
- route_weights: float32 [512, 8], P(('pool', 'grp', 'rep')), may hold values from 0.02 to 0.25
- w_gate: bfloat16 [64, 4096, 1536], P(('grp', 'rep'), None, 'pool'), may hold values from -0.09375 to 0.09375
- w_up: bfloat16 [64, 4096, 1536], P(('grp', 'rep'), None, 'pool'), may hold values from -0.09375 to 0.09375
- w_down: bfloat16 [64, 1536, 4096], P(('grp', 'rep'), 'pool'), may hold values from -0.15625 to 0.15625
Outputs:
- mid_rows: bfloat16 [512, 4096], P(('pool', 'grp', 'rep'))
- expert_mix: bfloat16 [512, 4096], P(('pool', 'grp', 'rep'))
Inputs may be any that keep to these rules, and one draw needn't show every extreme that they name: `routes`: each row names 8 different experts. In the rows of one device each expert is named by no row or by exactly 2 rows, and one expert, the same on every device, is named by 2 rows on every device.
All inputs are finite; a program needn't handle non-finite values.
Results may differ from a plain program's by a relative error of at most 0.027.
Values may be sent and summed in bfloat16 or wider, within the bound.
A program may use at most 128 MiB of HBM per device.

v0:
```python
import jax
import jax.numpy as jnp
from jax import lax
from jax.sharding import PartitionSpec as P

HEAD_DIM = 128


def joined(value, axis, combine):
    everything = jax.tree.map(lambda part: lax.all_gather(part, axis), value)
    initial = jax.tree.map(lambda part: part[0], everything)

    def hop(k, so_far):
        return combine(so_far, jax.tree.map(lambda part: part[k], everything))

    return lax.fori_loop(1, lax.axis_size(axis), hop, initial)


def expert_apply(rows_in, gate_w, up_w, down_w):
    gate_proj = jnp.dot(rows_in, gate_w, preferred_element_type=jnp.float32)
    upper = jnp.dot(rows_in, up_w, preferred_element_type=jnp.float32)
    activated = (jax.nn.silu(gate_proj) * upper).astype(jnp.bfloat16)
    return jnp.dot(activated, down_w, preferred_element_type=jnp.float32)


def softmax_merge(earlier, later):
    first_top, first_total, first_out = earlier
    second_top, second_total, second_out = later
    joint_top = jnp.maximum(first_top, second_top)
    first_scale = jnp.exp(first_top - joint_top)
    second_scale = jnp.exp(second_top - joint_top)
    joint_total = first_total * first_scale + second_total * second_scale
    joint_out = first_out * first_scale[..., None] + second_out * second_scale[..., None]
    return (joint_top, joint_total, joint_out)


def per_device(
    queries,
    keys,
    values,
    hidden_in,
    o_weight,
    norm_gain,
    routes,
    route_weights,
    w_gate,
    w_up,
    w_down,
):
    kv_local = keys.shape[1] // HEAD_DIM
    heads_local = queries.shape[1] // HEAD_DIM
    group_size = heads_local // kv_local
    batch_rows = queries.shape[0]
    key_span = keys.shape[0]
    per_block = min(4, group_size)
    blocks = group_size // per_block
    score_scale = HEAD_DIM ** (-0.5)
    query_blocks = jnp.moveaxis(
        queries.reshape(batch_rows, kv_local, blocks, per_block, HEAD_DIM), 2, 0
    )
    key_heads = keys.reshape(key_span, kv_local, HEAD_DIM)
    value_heads = values.reshape(key_span, kv_local, HEAD_DIM)

    def local_part(query_block):
        scores = (
            jnp.einsum("rkhd,pkd->rkhp", query_block, key_heads, preferred_element_type=jnp.float32)
            * score_scale
        )
        top_score = jnp.max(scores, axis=-1)
        exp_scores = jnp.exp(scores - top_score[..., None])
        exp_total = jnp.sum(exp_scores, axis=-1)
        weighted = jnp.einsum(
            "rkhp,pkd->rkhd",
            exp_scores.astype(jnp.bfloat16),
            value_heads,
            preferred_element_type=jnp.float32,
        )
        return (top_score, exp_total, weighted)

    top_part, total_part, value_part = lax.map(local_part, query_blocks)
    top_score, exp_total, weighted = joined(
        (top_part, total_part, value_part), "rep", softmax_merge
    )
    attention = (weighted / exp_total[..., None]).astype(jnp.bfloat16)
    attention = jnp.moveaxis(attention, 0, 2).reshape(batch_rows, heads_local * HEAD_DIM)
    head_total = lax.psum_scatter(
        jnp.dot(attention, o_weight, preferred_element_type=jnp.float32),
        "grp",
        scatter_dimension=0,
        tiled=True,
    )
    attn_proj = head_total.astype(jnp.bfloat16)
    full_rows = lax.all_to_all(attn_proj, "rep", split_axis=0, concat_axis=1, tiled=True)
    mid_rows = (hidden_in.astype(jnp.float32) + full_rows.astype(jnp.float32)).astype(jnp.bfloat16)
    mid_wide = lax.optimization_barrier(mid_rows).astype(jnp.float32)
    inverse = lax.rsqrt(jnp.mean(mid_wide * mid_wide, axis=-1, keepdims=True) + 1e-06)
    normed = (mid_wide * inverse * norm_gain.astype(jnp.float32)).astype(jnp.bfloat16)
    row_dev, topk = routes.shape
    model_width = hidden_in.shape[1]
    group_count = lax.axis_size("grp")
    rep_count = lax.axis_size("rep")
    experts = group_count * rep_count
    capacity = max(2, 2 * row_dev * topk // experts)
    flat_routes = routes.reshape(-1)
    member = (flat_routes[:, None] == jnp.arange(experts, dtype=jnp.int32)[None, :]).astype(
        jnp.int32
    )
    position = jnp.sum(jnp.cumsum(member, axis=0) * member, axis=1) - 1
    slot_index = flat_routes * capacity + position
    chooser = jnp.any(
        jnp.arange(experts * capacity, dtype=jnp.int32)[:, None, None]
        == slot_index.reshape(row_dev, topk)[None, :, :],
        axis=2,
    ).astype(jnp.bfloat16)
    outgoing = jnp.dot(chooser, normed, preferred_element_type=jnp.float32).astype(jnp.bfloat16)
    arrived = lax.all_to_all(
        outgoing.reshape(experts, capacity, model_width),
        ("grp", "rep"),
        split_axis=0,
        concat_axis=0,
        tiled=True,
    )
    sources = arrived.shape[0]
    slots_here = arrived.shape[1]
    combined = expert_apply(
        lax.all_gather(arrived.reshape(-1, model_width), "pool", axis=0, tiled=True),
        w_gate[0],
        w_up[0],
        w_down[0],
    )
    served = (
        lax.psum_scatter(combined, "pool", scatter_dimension=0, tiled=True)
        .astype(jnp.bfloat16)
        .reshape(sources, slots_here, model_width)
    )
    returned = lax.all_to_all(served, ("grp", "rep"), split_axis=0, concat_axis=0, tiled=True)
    returned = returned.reshape(-1, model_width)
    picked = jnp.take(returned, slot_index, axis=0).reshape(row_dev, topk, model_width)
    expert_mix = jnp.sum(route_weights[..., None] * picked.astype(jnp.float32), axis=1).astype(
        jnp.bfloat16
    )
    return (mid_rows, expert_mix)


def solution(mesh):
    return jax.shard_map(
        per_device,
        mesh=mesh,
        in_specs=(
            P("pool", "grp"),
            P("rep", "grp"),
            P("rep", "grp"),
            P(("pool", "grp", "rep"), None),
            P("grp", "rep"),
            P(),
            P(("pool", "grp", "rep"), None),
            P(("pool", "grp", "rep"), None),
            P(("grp", "rep"), None, "pool"),
            P(("grp", "rep"), None, "pool"),
            P(("grp", "rep"), "pool", None),
        ),
        out_specs=(P(("pool", "grp", "rep"), None), P(("pool", "grp", "rep"), None)),
        check_vma=False,
    )
```

profile of v0, /device:TPU:1, one launch (start us, length us, event | category | flops | bytes accessed | tf_op | source)
XLA Modules:
  0.0 552.0 jit_solution(18415080097469255329)
XLA Ops:
  8.9 13.8 %while.33 = (s32[]{:T(128)}, f32[4,256,1,4]{1,3,2,0:T(4,128)S(1)}, f32[4,256,1,4]{1,3,2,0:T(4,128)S(1)}, f32[4,256,1,4,128]{4,1,3,2,0:T(8,128)}, bf16[4,256,1,4,...) while((s32[]{:T(128)}, f32[4,256,1,4]{1,3,2,0:T(4,128)S(1)}, ...), condition=%wide.region_3.4_spmd, body=%wide.region_0.3_spmd.sunk | while | flops 545257472 | bytes 13926505 | solution.py:80
  22.7 21.8 %all-gather = f32[64,256,1,4]{1,3,2,0:T(4,128)S(1)} all-gather(f32[4,256,1,4]{1,3,2,0:T(4,128)S(1)} %get-tuple-element.218), channel_id=2, replica_groups=mesh['pool'=2,'grp'=4,'rep'=16] {'rep'}, dimensions={0}, use_global_device_ids=true | all-gather | bytes 278528 | tf_op jit(solution)/shard_map/all_gather | solution.py:10
  44.5 21.0 %all-gather.1 = f32[64,256,1,4]{1,3,2,0:T(4,128)} all-gather(f32[4,256,1,4]{1,3,2,0:T(4,128)S(1)} %get-tuple-element.219), channel_id=3, replica_groups=mesh['pool'=2,'grp'=4,'rep'=16] {'rep'}, dimensions={0}, use_global_device_ids=true | all-gather | bytes 278528 | tf_op jit(solution)/shard_map/all_gather | solution.py:10
  66.4 158.6 %all-gather.8.cloned.1.call-done = f32[64,256,1,4,128]{4,1,3,2,0:T(8,128)} async-done(((f32[4,256,1,4,128]{4,1,3,2,0:T(8,128)}), f32[64,256,1,4,128]{4,1,3,2,0:T(8,128)}) %all-gather.8.cloned.1.call-update) | async-done | bytes 33554448 | tf_op jit(solution)/shard_map/all_gather | solution.py:10
  226.7 2.7 copy.39
  229.4 177.4 %while.34 = (s32[]{:T(128)}, f32[4,256,1,4]{1,3,2,0:T(4,128)S(1)}, f32[4,256,1,4]{1,3,2,0:T(4,128)S(1)}, f32[4,256,1,4,128]{4,3,2,1,0:T(4,128)}, f32[16,4,256,1,...) while((s32[]{:T(128)}, f32[4,256,1,4]{1,3,2,0:T(4,128)S(1)}, ...), condition=%wide.region_5.6_spmd, body=%wide.region_4.5_spmd.sunk | while | flops 1601541 | bytes 10797211 | solution.py:16
  230.2 1.7 constant_dynamic-slice_fusion.2
  234.0 7.2 %fusion.73 = f32[4,256,1,4,128]{4,3,2,1,0:T(4,128)} fusion(f32[1,4,256,1,4,128]{5,2,4,1,0,3:T(8,128)S(1)} %constant_dynamic-slice_fusion.2, f32[4,256,1,4,128]{4,3,2,1,0:T(4,128)} %get-tuple-element.435, f32[4,256,4]{2,1,0:T(8,128)} %copy.56, f32[4,256,4]{2,1,0:T(8,128)} %copy.57), kind=kLoop, calls=%fused_computation.23.clone.1 | loop fusion | flops 1572864 | bytes 6324224 | tf_op jit(solution)/shard_map/while/body/eval_jaxpr/add | solution.py:33
  242.0 1.7 constant_dynamic-slice_fusion.2
  245.8 7.2 %fusion.73 = f32[4,256,1,4,128]{4,3,2,1,0:T(4,128)} fusion(f32[1,4,256,1,4,128]{5,2,4,1,0,3:T(8,128)S(1)} %constant_dynamic-slice_fusion.2, f32[4,256,1,4,128]{4,3,2,1,0:T(4,128)} %get-tuple-element.435, f32[4,256,4]{2,1,0:T(8,128)} %copy.56, f32[4,256,4]{2,1,0:T(8,128)} %copy.57), kind=kLoop, calls=%fused_computation.23.clone.1 | loop fusion | flops 1572864 | bytes 6324224 | tf_op jit(solution)/shard_map/while/body/eval_jaxpr/add | solution.py:33
  253.8 1.7 constant_dynamic-slice_fusion.2
  257.6 7.2 %fusion.73 = f32[4,256,1,4,128]{4,3,2,1,0:T(4,128)} fusion(f32[1,4,256,1,4,128]{5,2,4,1,0,3:T(8,128)S(1)} %constant_dynamic-slice_fusion.2, f32[4,256,1,4,128]{4,3,2,1,0:T(4,128)} %get-tuple-element.435, f32[4,256,4]{2,1,0:T(8,128)} %copy.56, f32[4,256,4]{2,1,0:T(8,128)} %copy.57), kind=kLoop, calls=%fused_computation.23.clone.1 | loop fusion | flops 1572864 | bytes 6324224 | tf_op jit(solution)/shard_map/while/body/eval_jaxpr/add | solution.py:33
  265.6 1.7 constant_dynamic-slice_fusion.2
  269.4 7.2 %fusion.73 = f32[4,256,1,4,128]{4,3,2,1,0:T(4,128)} fusion(f32[1,4,256,1,4,128]{5,2,4,1,0,3:T(8,128)S(1)} %constant_dynamic-slice_fusion.2, f32[4,256,1,4,128]{4,3,2,1,0:T(4,128)} %get-tuple-element.435, f32[4,256,4]{2,1,0:T(8,128)} %copy.56, f32[4,256,4]{2,1,0:T(8,128)} %copy.57), kind=kLoop, calls=%fused_computation.23.clone.1 | loop fusion | flops 1572864 | bytes 6324224 | tf_op jit(solution)/shard_map/while/body/eval_jaxpr/add | solution.py:33
  277.5 1.7 constant_dynamic-slice_fusion.2
  281.3 7.2 %fusion.73 = f32[4,256,1,4,128]{4,3,2,1,0:T(4,128)} fusion(f32[1,4,256,1,4,128]{5,2,4,1,0,3:T(8,128)S(1)} %constant_dynamic-slice_fusion.2, f32[4,256,1,4,128]{4,3,2,1,0:T(4,128)} %get-tuple-element.435, f32[4,256,4]{2,1,0:T(8,128)} %copy.56, f32[4,256,4]{2,1,0:T(8,128)} %copy.57), kind=kLoop, calls=%fused_computation.23.clone.1 | loop fusion | flops 1572864 | bytes 6324224 | tf_op jit(solution)/shard_map/while/body/eval_jaxpr/add | solution.py:33
  289.3 1.7 constant_dynamic-slice_fusion.2
  293.1 7.2 %fusion.73 = f32[4,256,1,4,128]{4,3,2,1,0:T(4,128)} fusion(f32[1,4,256,1,4,128]{5,2,4,1,0,3:T(8,128)S(1)} %constant_dynamic-slice_fusion.2, f32[4,256,1,4,128]{4,3,2,1,0:T(4,128)} %get-tuple-element.435, f32[4,256,4]{2,1,0:T(8,128)} %copy.56, f32[4,256,4]{2,1,0:T(8,128)} %copy.57), kind=kLoop, calls=%fused_computation.23.clone.1 | loop fusion | flops 1572864 | bytes 6324224 | tf_op jit(solution)/shard_map/while/body/eval_jaxpr/add | solution.py:33
  301.1 1.7 constant_dynamic-slice_fusion.2
  304.9 7.2 %fusion.73 = f32[4,256,1,4,128]{4,3,2,1,0:T(4,128)} fusion(f32[1,4,256,1,4,128]{5,2,4,1,0,3:T(8,128)S(1)} %constant_dynamic-slice_fusion.2, f32[4,256,1,4,128]{4,3,2,1,0:T(4,128)} %get-tuple-element.435, f32[4,256,4]{2,1,0:T(8,128)} %copy.56, f32[4,256,4]{2,1,0:T(8,128)} %copy.57), kind=kLoop, calls=%fused_computation.23.clone.1 | loop fusion | flops 1572864 | bytes 6324224 | tf_op jit(solution)/shard_map/while/body/eval_jaxpr/add | solution.py:33
  313.0 1.7 constant_dynamic-slice_fusion.2
  316.7 7.2 %fusion.73 = f32[4,256,1,4,128]{4,3,2,1,0:T(4,128)} fusion(f32[1,4,256,1,4,128]{5,2,4,1,0,3:T(8,128)S(1)} %constant_dynamic-slice_fusion.2, f32[4,256,1,4,128]{4,3,2,1,0:T(4,128)} %get-tuple-element.435, f32[4,256,4]{2,1,0:T(8,128)} %copy.56, f32[4,256,4]{2,1,0:T(8,128)} %copy.57), kind=kLoop, calls=%fused_computation.23.clone.1 | loop fusion | flops 1572864 | bytes 6324224 | tf_op jit(solution)/shard_map/while/body/eval_jaxpr/add | solution.py:33
  324.8 1.7 constant_dynamic-slice_fusion.2
  328.6 7.2 %fusion.73 = f32[4,256,1,4,128]{4,3,2,1,0:T(4,128)} fusion(f32[1,4,256,1,4,128]{5,2,4,1,0,3:T(8,128)S(1)} %constant_dynamic-slice_fusion.2, f32[4,256,1,4,128]{4,3,2,1,0:T(4,128)} %get-tuple-element.435, f32[4,256,4]{2,1,0:T(8,128)} %copy.56, f32[4,256,4]{2,1,0:T(8,128)} %copy.57), kind=kLoop, calls=%fused_computation.23.clone.1 | loop fusion | flops 1572864 | bytes 6324224 | tf_op jit(solution)/shard_map/while/body/eval_jaxpr/add | solution.py:33
  336.6 1.7 constant_dynamic-slice_fusion.2
  340.4 7.2 %fusion.73 = f32[4,256,1,4,128]{4,3,2,1,0:T(4,128)} fusion(f32[1,4,256,1,4,128]{5,2,4,1,0,3:T(8,128)S(1)} %constant_dynamic-slice_fusion.2, f32[4,256,1,4,128]{4,3,2,1,0:T(4,128)} %get-tuple-element.435, f32[4,256,4]{2,1,0:T(8,128)} %copy.56, f32[4,256,4]{2,1,0:T(8,128)} %copy.57), kind=kLoop, calls=%fused_computation.23.clone.1 | loop fusion | flops 1572864 | bytes 6324224 | tf_op jit(solution)/shard_map/while/body/eval_jaxpr/add | solution.py:33
  348.4 1.7 constant_dynamic-slice_fusion.2
  352.2 7.2 %fusion.73 = f32[4,256,1,4,128]{4,3,2,1,0:T(4,128)} fusion(f32[1,4,256,1,4,128]{5,2,4,1,0,3:T(8,128)S(1)} %constant_dynamic-slice_fusion.2, f32[4,256,1,4,128]{4,3,2,1,0:T(4,128)} %get-tuple-element.435, f32[4,256,4]{2,1,0:T(8,128)} %copy.56, f32[4,256,4]{2,1,0:T(8,128)} %copy.57), kind=kLoop, calls=%fused_computation.23.clone.1 | loop fusion | flops 1572864 | bytes 6324224 | tf_op jit(solution)/shard_map/while/body/eval_jaxpr/add | solution.py:33
  360.3 1.7 constant_dynamic-slice_fusion.2
  364.1 7.2 %fusion.73 = f32[4,256,1,4,128]{4,3,2,1,0:T(4,128)} fusion(f32[1,4,256,1,4,128]{5,2,4,1,0,3:T(8,128)S(1)} %constant_dynamic-slice_fusion.2, f32[4,256,1,4,128]{4,3,2,1,0:T(4,128)} %get-tuple-element.435, f32[4,256,4]{2,1,0:T(8,128)} %copy.56, f32[4,256,4]{2,1,0:T(8,128)} %copy.57), kind=kLoop, calls=%fused_computation.23.clone.1 | loop fusion | flops 1572864 | bytes 6324224 | tf_op jit(solution)/shard_map/while/body/eval_jaxpr/add | solution.py:33
  372.1 1.7 constant_dynamic-slice_fusion.2
  375.9 7.2 %fusion.73 = f32[4,256,1,4,128]{4,3,2,1,0:T(4,128)} fusion(f32[1,4,256,1,4,128]{5,2,4,1,0,3:T(8,128)S(1)} %constant_dynamic-slice_fusion.2, f32[4,256,1,4,128]{4,3,2,1,0:T(4,128)} %get-tuple-element.435, f32[4,256,4]{2,1,0:T(8,128)} %copy.56, f32[4,256,4]{2,1,0:T(8,128)} %copy.57), kind=kLoop, calls=%fused_computation.23.clone.1 | loop fusion | flops 1572864 | bytes 6324224 | tf_op jit(solution)/shard_map/while/body/eval_jaxpr/add | solution.py:33
  383.9 1.7 constant_dynamic-slice_fusion.2
  387.7 7.2 %fusion.73 = f32[4,256,1,4,128]{4,3,2,1,0:T(4,128)} fusion(f32[1,4,256,1,4,128]{5,2,4,1,0,3:T(8,128)S(1)} %constant_dynamic-slice_fusion.2, f32[4,256,1,4,128]{4,3,2,1,0:T(4,128)} %get-tuple-element.435, f32[4,256,4]{2,1,0:T(8,128)} %copy.56, f32[4,256,4]{2,1,0:T(8,128)} %copy.57), kind=kLoop, calls=%fused_computation.23.clone.1 | loop fusion | flops 1572864 | bytes 6324224 | tf_op jit(solution)/shard_map/while/body/eval_jaxpr/add | solution.py:33
  395.7 1.7 constant_dynamic-slice_fusion.2
  399.5 7.2 %fusion.73 = f32[4,256,1,4,128]{4,3,2,1,0:T(4,128)} fusion(f32[1,4,256,1,4,128]{5,2,4,1,0,3:T(8,128)S(1)} %constant_dynamic-slice_fusion.2, f32[4,256,1,4,128]{4,3,2,1,0:T(4,128)} %get-tuple-element.435, f32[4,256,4]{2,1,0:T(8,128)} %copy.56, f32[4,256,4]{2,1,0:T(8,128)} %copy.57), kind=kLoop, calls=%fused_computation.23.clone.1 | loop fusion | flops 1572864 | bytes 6324224 | tf_op jit(solution)/shard_map/while/body/eval_jaxpr/add | solution.py:33
  406.8 1.9 copy.43
  410.5 17.9 %reduce-scatter.3.cloned.1.call-done = f32[64,256]{1,0:T(8,128)} async-done(((f32[256,256]{1,0:T(8,128)}), f32[64,256]{1,0:T(8,128)}) %reduce-scatter.3.cloned.1.call-update) | async-done | bytes 65552 | tf_op jit(solution)/shard_map/reduce_scatter | solution.py:86
  429.8 6.7 %all-to-all-start = ((bf16[16,4,256]{2,1,0:T(4,128)(2,1)}), bf16[16,4,256]{2,1,0:T(4,128)(2,1)S(1)}, u32[]{:S(2)}, u32[]{:S(2)}) async-start(bf16[16,4,256]{2,1,0:T(4,128)(2,1)} %all_to_all.16), calls=%async_computation.1 | async-start | bytes 65536 | tf_op jit(solution)/shard_map/all_to_all | solution.py:93
  436.6 6.3 %all-to-all-done = bf16[16,4,256]{2,1,0:T(4,128)(2,1)S(1)} async-done(((bf16[16,4,256]{2,1,0:T(4,128)(2,1)}), bf16[16,4,256]{2,1,0:T(4,128)(2,1)S(1)}, u32[]{:S(2)}, u32[]{:S(2)}) %all-to-all-start) | async-done | bytes 32800 | tf_op jit(solution)/shard_map/all_to_all | solution.py:93
  444.4 18.6 %all_to_all.23 = bf16[64,2,4096]{2,1,0:T(2,128)(2,1)S(1)} all-to-all(bf16[64,2,4096]{2,1,0:T(2,128)(2,1)S(1)} %reshape.169), channel_id=1, replica_groups=mesh['pool'=2,'grp'=4,'rep'=16] {'grp','rep'}, dimensions={0} | all-to-all | bytes 2097152 | tf_op jit(solution)/shard_map/all_to_all | solution.py:116
  464.4 14.3 %all-gather.6.cloned.1.call-done = bf16[256,4096]{1,0:T(8,128)(2,1)} async-done(((bf16[128,4096]{1,0:T(8,128)(2,1)}), bf16[256,4096]{1,0:T(8,128)(2,1)}) %all-gather.6.cloned.1.call-update) | async-done | bytes 2097168 | tf_op jit(solution)/shard_map/all_gather | solution.py:126
  478.8 6.2 %fusion.31 = f32[256,768]{1,0:T(8,128)} fusion(bf16[256,4096]{1,0:T(8,128)(2,1)} %all-gather.6.cloned.1.call-done, bf16[1,4096,768]{2,1,0:T(8,128)(2,1)} %param.23), kind=kOutput, calls=%fused_computation.37 | convolution fusion | flops 1610612736 | bytes 9175040 | tf_op jit(solution)/shard_map/dot_general | solution.py:20
  485.0 11.3 %fusion.27 = f32[256,4096]{1,0:T(8,128)} fusion(bf16[1,768,4096]{2,1,0:T(8,128)(2,1)} %param.25, bf16[256,4096]{1,0:T(8,128)(2,1)S(1)} %copy-done.8, bf16[1,4096,768]{2,1,0:T(8,128)(2,1)} %param.24, f32[256,768]{1,0:T(8,128)} %fusion.31), kind=kOutput, calls=%fused_computation.33 | convolution fusion | flops 3222405120 | bytes 19660800 | tf_op jit(solution)/shard_map/dot_general | solution.py:23
  496.4 16.2 %reduce-scatter.5.cloned.1.call-done = f32[128,4096]{1,0:T(8,128)} async-done(((f32[256,4096]{1,0:T(8,128)}), f32[128,4096]{1,0:T(8,128)}) %reduce-scatter.5.cloned.1.call-update) | async-done | bytes 2097168 | tf_op jit(solution)/shard_map/reduce_scatter | solution.py:132
  512.6 1.7 convert_element_type.65
  515.8 10.2 %all-to-all-start.2 = ((bf16[64,2,4096]{2,1,0:T(2,128)(2,1)}), bf16[64,2,4096]{2,1,0:T(2,128)(2,1)S(1)}, u32[]{:S(2)}, u32[]{:S(2)}) async-start(bf16[64,2,4096]{2,1,0:T(2,128)(2,1)} %reshape.171), calls=%async_computation.4 | async-start | bytes 2097152 | tf_op jit(solution)/shard_map/all_to_all | solution.py:136
  526.1 17.4 %all-to-all-done.2 = bf16[64,2,4096]{2,1,0:T(2,128)(2,1)S(1)} async-done(((bf16[64,2,4096]{2,1,0:T(2,128)(2,1)}), bf16[64,2,4096]{2,1,0:T(2,128)(2,1)S(1)}, u32[]{:S(2)}, u32[]{:S(2)}) %all-to-all-start.2) | async-done | bytes 1048608 | tf_op jit(solution)/shard_map/all_to_all | solution.py:136
  (153 shorter events, 70.0 us)
Async XLA Ops:
  7.2 401.8 %copy-start = (bf16[2048,256]{1,0:T(8,128)(2,1)S(1)}, bf16[2048,256]{1,0:T(8,128)(2,1)}, u32[]{:S(2)}) copy-start(bf16[2048,256]{1,0:T(8,128)(2,1)} %param.19) | copy-start | bytes 3145732
  7.2 1.7 copy-start.1
  7.2 1.7 copy-start.2
  7.2 217.9 %all-gather.8.cloned.1.call-start = ((), (), s32[]{:S(2)}) async-start(), calls=%async_computation.8 | async-start | bytes 35651584 | tf_op jit(solution)/shard_map/all_gather | solution.py:10
  22.6 43.6 %copy-start.5 = (s32[4,8]{1,0:T(4,128)S(1)}, s32[4,8]{1,0:T(4,128)}, u32[]{:S(2)}) copy-start(s32[4,8]{1,0:T(4,128)} %param.21) | copy-start | bytes 388
  22.7 405.6 %reduce-scatter.3.cloned.1.call-start = ((), (), s32[]{:S(2)}) async-start(), calls=%async_computation.5 | async-start | bytes 327680 | tf_op jit(solution)/shard_map/reduce_scatter | solution.py:86
  225.1 1.6 slice-start
  408.9 27.7 %copy-start.6 = (bf16[4096]{0:T(1024)(128)(2,1)S(1)}, bf16[4096]{0:T(1024)(128)(2,1)}, u32[]{:S(2)}) copy-start(bf16[4096]{0:T(1024)(128)(2,1)} %param.20) | copy-start | bytes 24580
  408.9 34.0 %copy-start.4 = (bf16[4,4096]{1,0:T(4,128)(2,1)S(1)}, bf16[4,4096]{1,0:T(4,128)(2,1)}, u32[]{:S(2)}) copy-start(bf16[4,4096]{1,0:T(4,128)(2,1)} %param.18) | copy-start | bytes 98308
  429.8 13.1 %all-to-all-start = ((bf16[16,4,256]{2,1,0:T(4,128)(2,1)}), bf16[16,4,256]{2,1,0:T(4,128)(2,1)S(1)}, u32[]{:S(2)}, u32[]{:S(2)}) async-start(bf16[16,4,256]{2,1,0:T(4,128)(2,1)} %all_to_all.16), calls=%async_computation.1 | async-start | bytes 65536 | tf_op jit(solution)/shard_map/all_to_all | solution.py:93
  436.5 42.3 %all-gather.6.cloned.1.call-start = ((), (), s32[]{:S(2)}) async-start(), calls=%async_computation.6 | async-start | bytes 3145728 | tf_op jit(solution)/shard_map/all_gather | solution.py:126
  443.0 20.0 %copy-start.3 = (bf16[4,4096]{1,0:T(4,128)(2,1)}, bf16[4,4096]{1,0:T(4,128)(2,1)S(1)}, u32[]{:S(2)}) copy-start(bf16[4,4096]{1,0:T(4,128)(2,1)S(1)} %add_convert_fusion) | copy-start | bytes 98308
  464.2 48.4 %reduce-scatter.5.cloned.1.call-start = ((), (), s32[]{:S(2)}) async-start(), calls=%async_computation.7 | async-start | bytes 6291456 | tf_op jit(solution)/shard_map/reduce_scatter | solution.py:132
  478.8 6.2 %copy-start.8 = (bf16[256,4096]{1,0:T(8,128)(2,1)S(1)}, bf16[256,4096]{1,0:T(8,128)(2,1)}, u32[]{:S(2)}) copy-start(bf16[256,4096]{1,0:T(8,128)(2,1)} %all-gather.6.cloned.1.call-done) | copy-start | bytes 6291460
  515.8 27.7 %all-to-all-start.2 = ((bf16[64,2,4096]{2,1,0:T(2,128)(2,1)}), bf16[64,2,4096]{2,1,0:T(2,128)(2,1)S(1)}, u32[]{:S(2)}, u32[]{:S(2)}) async-start(bf16[64,2,4096]{2,1,0:T(2,128)(2,1)} %reshape.171), calls=%async_computation.4 | async-start | bytes 2097152 | tf_op jit(solution)/shard_map/all_to_all | solution.py:136
  526.0 18.6 %copy-start.7 = (f32[4,8]{1,0:T(4,128)S(1)}, f32[4,8]{1,0:T(4,128)}, u32[]{:S(2)}) copy-start(f32[4,8]{1,0:T(4,128)} %param.22) | copy-start | bytes 388
Sparse Core Ops, SparseCore 0:
  22.8 202.2 all-gather.7
  410.3 17.9 reduce-scatter.2
  464.3 14.4 all-gather.5
  496.5 16.0 reduce-scatter.4
where the time goes:
time: 556 us; the launch traced here: 552 us
  waiting for transfers between devices  231 us (42%)
  other arithmetic  128 us (23%)
  local copies, waits for them, and re-layouts  70.9 us (13%)
  blocking collectives  61.4 us (11%)
  matrix products  29.2 us (5%)
  starting transfers between devices  17.2 us (3%)
  between operations  14 us (3%)
    all_gather x1, waiting for transfers between devices, joined(): everything = jax.tree.map(lambda part: lax.all_gather(part, axis), value)  159 us
    add x15, other arithmetic, softmax_merge(): first_out * first_scale[..., None] + second_out * second_scale[..., None]  109 us
    all_gather x2, blocking collectives, joined(): everything = jax.tree.map(lambda part: lax.all_gather(part, axis), value)  42.8 us
    dynamic_slice x15, local copies, waits for them, and re-layouts, hop(): return combine(so_far, jax.tree.map(lambda part: part[k], everything))  26.1 us
    all_to_all x1, blocking collectives, per_device(): lax.all_to_all(outgoing.reshape(experts, capacity, model_width), ('grp',...  18.6 us
    reduce_scatter x1, waiting for transfers between devices, per_device(): lax.psum_scatter(jnp.dot(attention, o_weight, preferred_element_type=jnp....  17.9 us
    all_to_all x1, waiting for transfers between devices, per_device(): lax.all_to_all(served, ('grp', 'rep'), split_axis=0, concat_axis=0, tiled...  17.4 us
    reduce_scatter x1, waiting for transfers between devices, per_device(): lax.psum_scatter(combined, 'pool', scatter_dimension=0, tiled=True)  16.2 us
  transfers between devices with their start and end apart: 6, of which 6 were waited for; matrix products, arithmetic and copies ran while one was open for 0% of the time, Pallas kernels for 0%

commit v1 on v0

--- a/solution.py
+++ b/solution.py
@@ -6,32 +6,11 @@
 HEAD_DIM = 128
 
 
-def joined(value, axis, combine):
-    everything = jax.tree.map(lambda part: lax.all_gather(part, axis), value)
-    initial = jax.tree.map(lambda part: part[0], everything)
-
-    def hop(k, so_far):
-        return combine(so_far, jax.tree.map(lambda part: part[k], everything))
-
-    return lax.fori_loop(1, lax.axis_size(axis), hop, initial)
-
-
 def expert_apply(rows_in, gate_w, up_w, down_w):
     gate_proj = jnp.dot(rows_in, gate_w, preferred_element_type=jnp.float32)
     upper = jnp.dot(rows_in, up_w, preferred_element_type=jnp.float32)
     activated = (jax.nn.silu(gate_proj) * upper).astype(jnp.bfloat16)
     return jnp.dot(activated, down_w, preferred_element_type=jnp.float32)
-
-
-def softmax_merge(earlier, later):
-    first_top, first_total, first_out = earlier
-    second_top, second_total, second_out = later
-    joint_top = jnp.maximum(first_top, second_top)
-    first_scale = jnp.exp(first_top - joint_top)
-    second_scale = jnp.exp(second_top - joint_top)
-    joint_total = first_total * first_scale + second_total * second_scale
-    joint_out = first_out * first_scale[..., None] + second_out * second_scale[..., None]
-    return (joint_top, joint_total, joint_out)
 
 
 def per_device(
@@ -78,11 +57,29 @@
         return (top_score, exp_total, weighted)
 
     top_part, total_part, value_part = lax.map(local_part, query_blocks)
-    top_score, exp_total, weighted = joined(
-        (top_part, total_part, value_part), "rep", softmax_merge
+    rep_size = lax.axis_size("rep")
+    share = batch_rows // rep_size
+    rows_heads = share * heads_local
+
+    def by_peer(part):
+        part = jnp.moveaxis(part, 0, 2)
+        return part.reshape((rep_size, rows_heads) + part.shape[4:])
+
+    stats = jnp.stack([by_peer(top_part), by_peer(total_part)], axis=1)
+    payload = jnp.concatenate(
+        [by_peer(value_part), stats.reshape(rep_size, -1, HEAD_DIM)], axis=1
     )
-    attention = (weighted / exp_total[..., None]).astype(jnp.bfloat16)
-    attention = jnp.moveaxis(attention, 0, 2).reshape(batch_rows, heads_local * HEAD_DIM)
+    payload = lax.all_to_all(payload, "rep", split_axis=0, concat_axis=0, tiled=True)
+    weighted = payload[:, :rows_heads]
+    stats = payload[:, rows_heads:].reshape(rep_size, 2, rows_heads)
+    joint_top = jnp.max(stats[:, 0], axis=0)
+    factors = jnp.exp(stats[:, 0] - joint_top)
+    exp_total = jnp.sum(stats[:, 1] * factors, axis=0)
+    weighted = jnp.sum(weighted * factors[..., None], axis=0)
+    attention = (weighted / exp_total[:, None]).astype(jnp.bfloat16)
+    attention = lax.all_gather(
+        attention.reshape(share, heads_local * HEAD_DIM), "rep", axis=0, tiled=True
+    )
     head_total = lax.psum_scatter(
         jnp.dot(attention, o_weight, preferred_element_type=jnp.float32),
         "grp",
@@ -102,10 +99,9 @@
     experts = group_count * rep_count
     capacity = max(2, 2 * row_dev * topk // experts)
     flat_routes = routes.reshape(-1)
-    member = (flat_routes[:, None] == jnp.arange(experts, dtype=jnp.int32)[None, :]).astype(
-        jnp.int32
-    )
-    position = jnp.sum(jnp.cumsum(member, axis=0) * member, axis=1) - 1
+    order = jnp.arange(flat_routes.shape[0], dtype=jnp.int32)
+    same_before = (flat_routes[:, None] == flat_routes[None, :]) & (order[None, :] < order[:, None])
+    position = jnp.sum(same_before.astype(jnp.int32), axis=1)
     slot_index = flat_routes * capacity + position
     chooser = jnp.any(
         jnp.arange(experts * capacity, dtype=jnp.int32)[:, None, None]

time: 556 us -> 257 us (0.46)
  other arithmetic: 128 us -> 9.24 us
  waiting for transfers between devices: 231 us -> 114 us
  local copies, waits for them, and re-layouts: 70.9 us -> 11.9 us
  blocking collectives: 61.4 us -> 55.1 us
    all_gather x1, waiting for transfers between devices: 159 us -> 40.8 us  [per_device(): lax.all_gather(attention.reshape(share, heads_local * HEAD_DIM), 'rep', a...]
    add x15 -> x0, other arithmetic: 109 us -> none  [softmax_merge(): first_out * first_scale[..., None] + second_out * second_scale[..., None]]
    all_gather x2 -> x0, blocking collectives: 42.8 us -> none  [joined(): everything = jax.tree.map(lambda part: lax.all_gather(part, axis), value)]
    all_to_all x0 -> x1, blocking collectives: none -> 36.5 us  [per_device(): lax.all_to_all(payload, 'rep', split_axis=0, concat_axis=0, tiled=True)]
    mul x30 -> x0, local copies, waits for them, and re-layouts: 30.7 us -> none  [the longest x15 15.5 us: softmax_merge(): second_out * second_scale[..., None]]
    dynamic_slice x15 -> x0, local copies, waits for them, and re-layouts: 26.1 us -> none  [hop(): return combine(so_far, jax.tree.map(lambda part: part[k], everything))]
    mul x30 -> x0, other arithmetic: 11.5 us -> none  [the longest x15 11.3 us: softmax_merge(): second_out * second_scale[..., None]]
where the time goes in v1:
time: 257 us; the launch traced here: 256 us
  waiting for transfers between devices  114 us (44%)
  blocking collectives  55.1 us (21%)
  matrix products  34.3 us (13%)
  starting transfers between devices  17.2 us (7%)
  between operations  14 us (5%)
  local copies, waits for them, and re-layouts  11.9 us (5%)
  other arithmetic  9.24 us (4%)
    all_gather x1, waiting for transfers between devices, per_device(): lax.all_gather(attention.reshape(share, heads_local * HEAD_DIM), 'rep', a...  40.8 us
    all_to_all x1, blocking collectives, per_device(): lax.all_to_all(payload, 'rep', split_axis=0, concat_axis=0, tiled=True)  36.5 us
    reduce_scatter x1, waiting for transfers between devices, per_device(): lax.psum_scatter(jnp.dot(attention, o_weight, preferred_element_type=jnp....  18.9 us
    all_to_all x1, blocking collectives, per_device(): lax.all_to_all(outgoing.reshape(experts, capacity, model_width), ('grp',...  18.6 us
    all_to_all x1, waiting for transfers between devices, per_device(): lax.all_to_all(served, ('grp', 'rep'), split_axis=0, concat_axis=0, tiled...  17.4 us
    reduce_scatter x1, waiting for transfers between devices, per_device(): lax.psum_scatter(combined, 'pool', scatter_dimension=0, tiled=True)  16.2 us
    all_gather x1, waiting for transfers between devices, per_device(): lax.all_gather(arrived.reshape(-1, model_width), 'pool', axis=0, tiled=True)  14.3 us
    dot_general x1, matrix products, expert_apply(): return jnp.dot(activated, down_w, preferred_element_type=jnp.float32)  11.3 us
  transfers between devices with their start and end apart: 6, of which 6 were waited for; matrix products, arithmetic and copies ran while one was open for 0% of the time, Pallas kernels for 0%

profile of v1, /device:TPU:1, one launch (start us, length us, event | category | flops | bytes accessed | tf_op | source)
XLA Modules:
  0.0 255.8 jit_solution(1512416310897008572)
XLA Ops:
  7.3 1.6 copy.23
  8.8 17.7 %while.14 = (s32[]{:T(128)}, f32[4,256,1,4]{1,3,2,0:T(4,128)S(1)}, f32[4,256,1,4]{1,3,2,0:T(4,128)S(1)}, f32[4,256,1,4,128]{4,1,3,2,0:T(8,128)}, bf16[4,256,1,4,...) while((s32[]{:T(128)}, f32[4,256,1,4]{1,3,2,0:T(4,128)S(1)}, ...), condition=%wide.region_3.4_spmd, body=%wide.region_0.3_spmd.sunk | while | flops 545257472 | bytes 14975609 | solution.py:59
  8.8 1.8 bitcast_reduce_fusion.2
  10.7 0.9 fusion.67
  11.6 1.6 fusion.68
  13.3 1.8 bitcast_reduce_fusion.2
  15.1 0.9 fusion.67
  16.0 1.7 fusion.68
  17.7 1.8 bitcast_reduce_fusion.2
  19.5 0.9 fusion.67
  20.5 1.7 fusion.68
  22.1 1.8 bitcast_reduce_fusion.2
  23.9 0.9 fusion.67
  24.9 1.7 fusion.68
  26.6 0.3 copy.26
  26.8 0.5 stack_reshape.6
  27.3 0.3 copy.27
  27.6 0.5 stack_reshape.7
  28.2 2.9 %copy.25 = f32[256,1,4,4,128]{4,3,2,0,1:T(4,128)S(1)} copy(f32[256,1,4,4,128]{4,0,3,1,2:T(8,128)} %bitcast.21) | data formatting | bytes 4194304 | tf_op jit(solution)/shard_map/transpose | solution.py:65
  31.1 0.2 pad_maximum_fusion
  31.3 36.5 %all_to_all.28 = f32[16,260,128]{2,1,0:T(8,128)S(1)} all-to-all(f32[16,260,128]{2,1,0:T(8,128)S(1)} %pad_maximum_fusion), channel_id=1, replica_groups=mesh['pool'=2,'grp'=4,'rep'=16] {'rep'}, dimensions={0} | all-to-all | bytes 4259840 | tf_op jit(solution)/shard_map/all_to_all | solution.py:72
  67.9 0.7 fusion.27
  68.8 0.7 fusion.37
  69.6 40.8 %all-gather.3.cloned.1.call-done = bf16[256,2048]{1,0:T(8,128)(2,1)} async-done(((bf16[16,2048]{1,0:T(8,128)(2,1)}), bf16[256,2048]{1,0:T(8,128)(2,1)}) %all-gather.3.cloned.1.call-update) | async-done | bytes 1048592 | tf_op jit(solution)/shard_map/all_gather | solution.py:80
  110.4 2.4 fusion.55
  112.9 0.2 convert_reduce_fusion
  113.2 18.9 %reduce-scatter.3.cloned.1.call-done = f32[64,256]{1,0:T(8,128)} async-done(((f32[256,256]{1,0:T(8,128)}), f32[64,256]{1,0:T(8,128)}) %reduce-scatter.3.cloned.1.call-update) | async-done | bytes 65552 | tf_op jit(solution)/shard_map/reduce_scatter | solution.py:83
  132.1 0.8 convert_element_type.55
  132.9 0.6 all_to_all.20
  133.5 6.7 %all-to-all-start.1 = ((bf16[16,4,256]{2,1,0:T(4,128)(2,1)}), bf16[16,4,256]{2,1,0:T(4,128)(2,1)S(1)}, u32[]{:S(2)}, u32[]{:S(2)}) async-start(bf16[16,4,256]{2,1,0:T(4,128)(2,1)} %all_to_all.20), calls=%async_computation.2 | async-start | bytes 65536 | tf_op jit(solution)/shard_map/all_to_all | solution.py:90
  140.4 6.3 %all-to-all-done.1 = bf16[16,4,256]{2,1,0:T(4,128)(2,1)S(1)} async-done(((bf16[16,4,256]{2,1,0:T(4,128)(2,1)}), bf16[16,4,256]{2,1,0:T(4,128)(2,1)S(1)}, u32[]{:S(2)}, u32[]{:S(2)}) %all-to-all-start.1) | async-done | bytes 32800 | tf_op jit(solution)/shard_map/all_to_all | solution.py:90
  146.8 0.1 fusion.38
  146.9 0.5 convolution_convert_fusion
  147.4 0.7 reshape.157
  148.1 18.6 %all_to_all.29 = bf16[64,2,4096]{2,1,0:T(2,128)(2,1)S(1)} all-to-all(bf16[64,2,4096]{2,1,0:T(2,128)(2,1)S(1)} %reshape.157), channel_id=1, replica_groups=mesh['pool'=2,'grp'=4,'rep'=16] {'grp','rep'}, dimensions={0} | all-to-all | bytes 2097152 | tf_op jit(solution)/shard_map/all_to_all | solution.py:112
  166.7 1.2 reshape.158
  168.0 0.2 reduce-scatter.5.cloned.1.call-start
  168.2 14.3 %all-gather.5.cloned.1.call-done = bf16[256,4096]{1,0:T(8,128)(2,1)} async-done(((bf16[128,4096]{1,0:T(8,128)(2,1)}), bf16[256,4096]{1,0:T(8,128)(2,1)}) %all-gather.5.cloned.1.call-update) | async-done | bytes 2097168 | tf_op jit(solution)/shard_map/all_gather | solution.py:122
  182.5 6.2 %fusion.25 = f32[256,768]{1,0:T(8,128)} fusion(bf16[256,4096]{1,0:T(8,128)(2,1)} %all-gather.5.cloned.1.call-done, bf16[1,4096,768]{2,1,0:T(8,128)(2,1)} %param.21), kind=kOutput, calls=%fused_computation.25 | convolution fusion | flops 1610612736 | bytes 9175040 | tf_op jit(solution)/shard_map/dot_general | solution.py:10
  188.8 11.3 %fusion.21 = f32[256,4096]{1,0:T(8,128)} fusion(bf16[1,768,4096]{2,1,0:T(8,128)(2,1)} %param.23, bf16[256,4096]{1,0:T(8,128)(2,1)S(1)} %copy-done.7, bf16[1,4096,768]{2,1,0:T(8,128)(2,1)} %param.22, f32[256,768]{1,0:T(8,128)} %fusion.25), kind=kOutput, calls=%fused_computation.21 | convolution fusion | flops 3222405120 | bytes 19660800 | tf_op jit(solution)/shard_map/dot_general | solution.py:13
  200.1 16.2 %reduce-scatter.5.cloned.1.call-done = f32[128,4096]{1,0:T(8,128)} async-done(((f32[256,4096]{1,0:T(8,128)}), f32[128,4096]{1,0:T(8,128)}) %reduce-scatter.5.cloned.1.call-update) | async-done | bytes 2097168 | tf_op jit(solution)/shard_map/reduce_scatter | solution.py:128
  216.3 1.7 convert_element_type.66
  218.0 1.5 reshape.159
  219.5 10.1 %all-to-all-start.3 = ((bf16[64,2,4096]{2,1,0:T(2,128)(2,1)}), bf16[64,2,4096]{2,1,0:T(2,128)(2,1)S(1)}, u32[]{:S(2)}, u32[]{:S(2)}) async-start(bf16[64,2,4096]{2,1,0:T(2,128)(2,1)} %reshape.159), calls=%async_computation.5 | async-start | bytes 2097152 | tf_op jit(solution)/shard_map/all_to_all | solution.py:132
  229.8 17.4 %all-to-all-done.3 = bf16[64,2,4096]{2,1,0:T(2,128)(2,1)S(1)} async-done(((bf16[64,2,4096]{2,1,0:T(2,128)(2,1)}), bf16[64,2,4096]{2,1,0:T(2,128)(2,1)S(1)}, u32[]{:S(2)}, u32[]{:S(2)}) %all-to-all-start.3) | async-done | bytes 1048608 | tf_op jit(solution)/shard_map/all_to_all | solution.py:132
  247.2 0.4 reshape.160
  247.6 0.7 gather_fusion
  248.4 0.9 multiply_reduce_fusion
  (58 shorter events, 1.1 us)
Async XLA Ops:
  7.2 103.2 %copy-start = (bf16[2048,256]{1,0:T(8,128)(2,1)S(1)}, bf16[2048,256]{1,0:T(8,128)(2,1)}, u32[]{:S(2)}) copy-start(bf16[2048,256]{1,0:T(8,128)(2,1)} %param.17) | copy-start | bytes 3145732
  7.2 103.2 %all-gather.3.cloned.1.call-start = ((), (), s32[]{:S(2)}) async-start(), calls=%async_computation.6 | async-start | bytes 1114112 | tf_op jit(solution)/shard_map/all_gather | solution.py:80
  8.8 2.8 %copy-start.1 = (bf16[1024,1,128]{2,0,1:T(8,128)(2,1)S(1)}, bf16[1024,1,128]{2,0,1:T(8,128)(2,1)}, u32[]{:S(2)}) copy-start(bf16[1024,1,128]{2,0,1:T(8,128)(2,1)} %get-tuple-element.156) | copy-start | bytes 786436 | tf_op jit(solution)/shard_map/while
  13.2 2.8 %copy-start.1 = (bf16[1024,1,128]{2,0,1:T(8,128)(2,1)S(1)}, bf16[1024,1,128]{2,0,1:T(8,128)(2,1)}, u32[]{:S(2)}) copy-start(bf16[1024,1,128]{2,0,1:T(8,128)(2,1)} %get-tuple-element.156) | copy-start | bytes 786436 | tf_op jit(solution)/shard_map/while
  17.7 2.8 %copy-start.1 = (bf16[1024,1,128]{2,0,1:T(8,128)(2,1)S(1)}, bf16[1024,1,128]{2,0,1:T(8,128)(2,1)}, u32[]{:S(2)}) copy-start(bf16[1024,1,128]{2,0,1:T(8,128)(2,1)} %get-tuple-element.156) | copy-start | bytes 786436 | tf_op jit(solution)/shard_map/while
  22.1 2.8 %copy-start.1 = (bf16[1024,1,128]{2,0,1:T(8,128)(2,1)S(1)}, bf16[1024,1,128]{2,0,1:T(8,128)(2,1)}, u32[]{:S(2)}) copy-start(bf16[1024,1,128]{2,0,1:T(8,128)(2,1)} %get-tuple-element.156) | copy-start | bytes 786436 | tf_op jit(solution)/shard_map/while
  31.3 81.5 %copy-start.4 = (s32[4,8]{1,0:T(4,128)S(1)}, s32[4,8]{1,0:T(4,128)}, u32[]{:S(2)}) copy-start(s32[4,8]{1,0:T(4,128)} %param.19) | copy-start | bytes 388
  31.3 109.1 %copy-start.5 = (bf16[4096]{0:T(1024)(128)(2,1)S(1)}, bf16[4096]{0:T(1024)(128)(2,1)}, u32[]{:S(2)}) copy-start(bf16[4096]{0:T(1024)(128)(2,1)} %param.18) | copy-start | bytes 24580
  67.8 79.0 %copy-start.3 = (bf16[4,4096]{1,0:T(4,128)(2,1)S(1)}, bf16[4,4096]{1,0:T(4,128)(2,1)}, u32[]{:S(2)}) copy-start(bf16[4,4096]{1,0:T(4,128)(2,1)} %param.16) | copy-start | bytes 98308
  69.5 62.6 %reduce-scatter.3.cloned.1.call-start = ((), (), s32[]{:S(2)}) async-start(), calls=%async_computation.7 | async-start | bytes 327680 | tf_op jit(solution)/shard_map/reduce_scatter | solution.py:83
  133.5 13.1 %all-to-all-start.1 = ((bf16[16,4,256]{2,1,0:T(4,128)(2,1)}), bf16[16,4,256]{2,1,0:T(4,128)(2,1)S(1)}, u32[]{:S(2)}, u32[]{:S(2)}) async-start(bf16[16,4,256]{2,1,0:T(4,128)(2,1)} %all_to_all.20), calls=%async_computation.2 | async-start | bytes 65536 | tf_op jit(solution)/shard_map/all_to_all | solution.py:90
  140.2 42.3 %all-gather.5.cloned.1.call-start = ((), (), s32[]{:S(2)}) async-start(), calls=%async_computation.8 | async-start | bytes 3145728 | tf_op jit(solution)/shard_map/all_gather | solution.py:122
  146.7 21.2 %copy-start.2 = (bf16[4,4096]{1,0:T(4,128)(2,1)}, bf16[4,4096]{1,0:T(4,128)(2,1)S(1)}, u32[]{:S(2)}) copy-start(bf16[4,4096]{1,0:T(4,128)(2,1)S(1)} %add_convert_fusion) | copy-start | bytes 98308
  168.0 48.3 %reduce-scatter.5.cloned.1.call-start = ((), (), s32[]{:S(2)}) async-start(), calls=%async_computation.9 | async-start | bytes 6291456 | tf_op jit(solution)/shard_map/reduce_scatter | solution.py:128
  182.5 6.2 %copy-start.7 = (bf16[256,4096]{1,0:T(8,128)(2,1)S(1)}, bf16[256,4096]{1,0:T(8,128)(2,1)}, u32[]{:S(2)}) copy-start(bf16[256,4096]{1,0:T(8,128)(2,1)} %all-gather.5.cloned.1.call-done) | copy-start | bytes 6291460
  218.0 30.4 %copy-start.6 = (f32[4,8]{1,0:T(4,128)S(1)}, f32[4,8]{1,0:T(4,128)}, u32[]{:S(2)}) copy-start(f32[4,8]{1,0:T(4,128)} %param.20) | copy-start | bytes 388
  219.5 27.7 %all-to-all-start.3 = ((bf16[64,2,4096]{2,1,0:T(2,128)(2,1)}), bf16[64,2,4096]{2,1,0:T(2,128)(2,1)S(1)}, u32[]{:S(2)}, u32[]{:S(2)}) async-start(bf16[64,2,4096]{2,1,0:T(2,128)(2,1)} %reshape.159), calls=%async_computation.5 | async-start | bytes 2097152 | tf_op jit(solution)/shard_map/all_to_all | solution.py:132
Sparse Core Ops, SparseCore 0:
  69.6 40.7 all-gather.2
  112.9 19.1 reduce-scatter.2
  168.1 14.3 all-gather.4
  200.2 16.0 reduce-scatter.4

commit v2 on v1

v2 whole, which is shorter than its diff:
```python
import functools

import jax
import jax.numpy as jnp
from jax import lax
from jax.experimental import pallas as pl
from jax.experimental.pallas import tpu as pltpu
from jax.sharding import PartitionSpec as P

HEAD_DIM = 128
CHUNKS = 8
SLOTS = 2
PAIR = CHUNKS * SLOTS
LOG2E = 1.4426950408889634
MESH = pl.DeviceIdType.MESH
BF = jnp.bfloat16
F32 = jnp.float32


def remote(src, dst, send, recv, where):
    return pltpu.make_async_remote_copy(
        src_ref=src,
        dst_ref=dst,
        send_sem=send,
        recv_sem=recv,
        device_id=where,
        device_id_type=MESH,
    )


def layer(
    G, R,
    q_hbm, k_hbm, v_hbm, ow_hbm, hidden_ref, gain_ref, sel_ref, comb_ref, wg_hbm, wu_hbm, wd_hbm,
    mid_ref, mix_ref,
    q_s, k_s, v_s, vt_s, ow_s, wg_s, wu_s, wd_s, load_sem,
    part_s, stat_s, part_r, stat_r, attn_s,
    proj_f, proj_s, proj_r, cols_s, cols_r,
    disp_s, disp_r, rows_s, act_s, half_s, half_r, sum_s, back_s, back_r,
    part_ss, part_rs, stat_ss, stat_rs, attn_ss, attn_rs,
    proj_ss, proj_rs, cols_ss, cols_rs, disp_ss, disp_rs,
    rows_ss, rows_rs, half_ss, half_rs, back_ss, back_rs,
):
    pool, grp, rep = lax.axis_index("pool"), lax.axis_index("grp"), lax.axis_index("rep")
    E = G * R
    me = grp * R + rep
    sibling = (1 - pool, grp, rep)

    loads = [
        pltpu.make_async_copy(src, dst, load_sem.at[i])
        for i, (src, dst) in enumerate(
            (
                (q_hbm, q_s),
                (k_hbm, k_s),
                (v_hbm, v_s),
                (ow_hbm, ow_s),
                (wg_hbm, wg_s),
                (wu_hbm, wu_s),
                (wd_hbm, wd_s),
            )
        )
    ]
    for load in loads:
        load.start()

    barrier = pltpu.get_barrier_semaphore()

    def greet(d, carry):
        there = lax.rem(me + d, E)
        pl.semaphore_signal(
            barrier, inc=1, device_id=(pool, there // R, lax.rem(there, R)), device_id_type=MESH
        )
        return carry

    lax.fori_loop(1, E, greet, 0)
    pl.semaphore_signal(barrier, inc=1, device_id=sibling, device_id_type=MESH)

    for load in loads[:3]:
        load.wait()
    vt_s[...] = v_s[...].astype(F32).T.astype(BF)
    pl.semaphore_wait(barrier, E)

    rows_all, width = q_s.shape
    heads = width // HEAD_DIM
    share = rows_all // R
    lanes = share * heads
    scale = LOG2E * HEAD_DIM ** (-0.5)

    def part_copy(s):
        where = (pool, grp, lax.rem(rep + 1 + s, R))
        return (
            remote(part_s.at[s], part_r.at[s], part_ss.at[s], part_rs.at[s], where),
            remote(stat_s.at[s], stat_r.at[s], stat_ss.at[s], stat_rs.at[s], where),
        )

    def attend(s, carry):
        peer = lax.rem(rep + 1 + s, R)
        block = pl.ds(pl.multiple_of(peer * share, share), share)
        query = jnp.concatenate(
            [q_s[block, h * HEAD_DIM : (h + 1) * HEAD_DIM] for h in range(heads)], axis=0
        )
        scores = lax.dot_general(
            k_s[...], query, (((1,), (1,)), ((), ())), preferred_element_type=F32
        )
        top = jnp.max(scores, axis=0, keepdims=True)
        probs = jnp.exp2((scores - top) * scale)
        total = jnp.sum(probs, axis=0, keepdims=True)
        part = jnp.dot(vt_s[...], probs.astype(BF), preferred_element_type=F32)
        part_s[s] = part.astype(BF)
        first = lax.broadcasted_iota(jnp.int32, (8, lanes), 0) < 4
        stat_s[s] = jnp.where(first, top, total)

        @pl.when(s < R - 1)
        def _():
            for copy in part_copy(s):
                copy.start()

        return carry

    lax.fori_loop(0, R, attend, 0)

    def part_wait(s, carry):
        for copy in part_copy(s):
            copy.wait()
        return carry

    lax.fori_loop(0, R - 1, part_wait, 0)

    stats = [stat_r[s] for s in range(R - 1)] + [stat_s[R - 1]]
    top = functools.reduce(jnp.maximum, [stat[0:1] for stat in stats])
    factors = [jnp.exp2((stat[0:1] - top) * scale) for stat in stats]
    total = functools.reduce(
        jnp.add, [stat[4:5] * factor for stat, factor in zip(stats, factors)]
    )
    weighted = part_s[R - 1].astype(F32) * factors[R - 1]
    for s in range(R - 1):
        weighted += part_r[s].astype(F32) * factors[s]
    attention = (weighted / total).T.astype(BF)
    mine = pl.ds(pl.multiple_of(rep * share, share), share)
    for h in range(heads):
        attn_s[mine, h * HEAD_DIM : (h + 1) * HEAD_DIM] = attention[h * share : (h + 1) * share]

    def attn_copy(d, block):
        at = attn_s.at[pl.ds(pl.multiple_of(block * share, share), share)]
        where = (pool, grp, lax.rem(rep + d, R))
        return remote(at, at, attn_ss.at[d - 1], attn_rs.at[d - 1], where)

    def attn_start(d, carry):
        attn_copy(d, rep).start()
        return carry

    def attn_recv(d, carry):
        attn_copy(d, lax.rem(rep - d + R, R)).wait_recv()
        return carry

    lax.fori_loop(1, R, attn_start, 0)
    lax.fori_loop(1, R, attn_recv, 0)
    loads[3].wait()
    proj_f[...] = jnp.dot(attn_s[...], ow_s[...], preferred_element_type=F32)

    tall = rows_all // G
    for g in range(G):
        proj_s[g] = proj_f[g * tall : (g + 1) * tall].astype(BF)

    def proj_copy(d):
        there = lax.rem(grp + d, G)
        return remote(
            proj_s.at[there], proj_r.at[d - 1], proj_ss.at[d - 1], proj_rs.at[d - 1],
            (pool, there, rep),
        )

    for d in range(1, G):
        proj_copy(d).start()
    summed = proj_f[pl.ds(pl.multiple_of(grp * tall, tall), tall), :]
    for d in range(1, G):
        proj_copy(d).wait_recv()
        summed = summed + proj_r[d - 1].astype(F32)
    summed = summed.astype(BF).astype(F32)
    few = tall // R
    for j in range(R):
        cols_s[j] = summed[j * few : (j + 1) * few]

    def cols_copy(d, src, dst):
        where = (pool, grp, lax.rem(rep + d, R))
        return remote(
            cols_s.at[src], cols_r.at[dst], cols_ss.at[d - 1], cols_rs.at[d - 1], where
        )

    def cols_start(d, carry):
        cols_copy(d, lax.rem(rep + d, R), rep).start()
        return carry

    def cols_recv(d, carry):
        cols_copy(d, rep, lax.rem(rep - d + R, R)).wait_recv()
        return carry

    lax.fori_loop(1, R, cols_start, 0)
    cols_r[rep] = cols_s[rep]
    lax.fori_loop(1, R, cols_recv, 0)

    projected = jnp.concatenate([cols_r[j] for j in range(R)], axis=1)
    mid = (hidden_ref[...].astype(F32) + projected).astype(BF)
    mid_ref[...] = mid
    wide = mid.astype(F32)
    inverse = lax.rsqrt(jnp.mean(wide * wide, axis=-1, keepdims=True) + 1e-06)
    normed = wide * inverse * gain_ref[...].astype(F32)
    piece = normed.shape[1] // CHUNKS
    pieces = jnp.concatenate(
        [normed[:, c * piece : (c + 1) * piece] for c in range(CHUNKS)], axis=0
    ).astype(BF)

    tile = R * PAIR

    def fill(t, carry):
        chosen = jnp.dot(
            sel_ref[pl.ds(pl.multiple_of(t * tile, tile), tile), :],
            pieces,
            preferred_element_type=F32,
        )
        disp_s[pl.ds(t * R, R)] = chosen.astype(BF).reshape(R, PAIR, piece)
        return carry

    lax.fori_loop(0, G, fill, 0)

    def pair_copy(src, dst, send, recv, d, a, b):
        there = lax.rem(me + d, E)
        where = (pool, there // R, lax.rem(there, R))
        return remote(src.at[a], dst.at[b], send.at[d - 1], recv.at[d - 1], where)

    def disp_copy(d, a, b):
        return pair_copy(disp_s, disp_r, disp_ss, disp_rs, d, a, b)

    def back_copy(d, a, b):
        return pair_copy(back_s, back_r, back_ss, back_rs, d, a, b)

    def disp_start(d, carry):
        disp_copy(d, lax.rem(me + d, E), me).start()
        return carry

    lax.fori_loop(1, E, disp_start, 0)
    disp_r[me] = disp_s[me]

    row = lax.broadcasted_iota(jnp.int32, (tile, tile), 0)
    col = lax.broadcasted_iota(jnp.int32, (tile, tile), 1)
    pairs = R * SLOTS

    def moved(i):
        return lax.rem(i, pairs) // SLOTS * PAIR + i // pairs * SLOTS + lax.rem(i, SLOTS)

    gather = jnp.where(col == moved(row), 1.0, 0.0).astype(BF)
    spread = jnp.where(row == moved(col), 1.0, 0.0).astype(BF)

    def rows_copy(i, t):
        at = rows_s.at[pl.ds(pl.multiple_of(pool * (E * SLOTS) + t * pairs, pairs), pairs)]
        return remote(at, at, rows_ss.at[i], rows_rs.at[i], sibling)

    def collect(i, carry):
        t = lax.rem(grp + i, G)

        def arrive(j, inner):
            source = t * R + j
            d = lax.rem(me - source + E, E)

            @pl.when(d != 0)
            def _():
                disp_copy(d, me, source).wait_recv()

            return inner

        lax.fori_loop(0, R, arrive, 0)
        arrived = disp_r[pl.ds(t * R, R)].reshape(tile, piece)
        ordered = jnp.dot(gather, arrived, preferred_element_type=F32).astype(BF)
        at = pl.ds(pl.multiple_of(pool * (E * SLOTS) + t * pairs, pairs), pairs)
        for c in range(CHUNKS):
            rows_s[at, c * piece : (c + 1) * piece] = ordered[c * pairs : (c + 1) * pairs]
        rows_copy(i, t).start()
        return carry

    lax.fori_loop(0, G, collect, 0)

    def rows_recv(i, carry):
        t = lax.rem(grp + i, G)
        at = rows_s.at[pl.ds(pl.multiple_of((1 - pool) * (E * SLOTS) + t * pairs, pairs), pairs)]
        remote(at, at, rows_ss.at[i], rows_rs.at[i], sibling).wait_recv()
        return carry

    lax.fori_loop(0, G, rows_recv, 0)
    loads[4].wait()
    loads[5].wait()
    hidden = act_s.shape[1]
    step = min(256, hidden)

    def expand(n, carry):
        at = pl.ds(pl.multiple_of(n * step, step), step)
        gate = jnp.dot(rows_s[...], wg_s[0, :, at], preferred_element_type=F32)
        upper = jnp.dot(rows_s[...], wu_s[0, :, at], preferred_element_type=F32)
        act_s[:, at] = (gate / (1.0 + jnp.exp(-gate)) * upper).astype(BF)
        return carry

    lax.fori_loop(0, hidden // step, expand, 0)
    loads[6].wait()
    side = E * SLOTS

    def half_copy(n):
        return remote(
            half_s.at[n, 1 - pool], half_r.at[n], half_ss.at[n], half_rs.at[n], sibling
        )

    def contract(n, carry):
        at = pl.ds(pl.multiple_of(n * piece, piece), piece)
        out = jnp.dot(act_s[...], wd_s[0, :, at], preferred_element_type=F32)
        half_s[n, 0] = out[:side].astype(BF)
        half_s[n, 1] = out[side:].astype(BF)
        half_copy(n).start()
        return carry

    lax.fori_loop(0, CHUNKS, contract, 0)

    def merge(n, carry):
        half_copy(n).wait_recv()
        sum_s[n] = (half_s[n, pool].astype(F32) + half_r[n].astype(F32)).astype(BF)
        return carry

    lax.fori_loop(0, CHUNKS, merge, 0)

    def give_back(i, carry):
        t = lax.rem(grp + i, G)
        at = pl.ds(pl.multiple_of(t * pairs, pairs), pairs)
        stacked = sum_s[:, at, :].reshape(tile, piece)
        out = jnp.dot(spread, stacked, preferred_element_type=F32).astype(BF)
        back_s[pl.ds(t * R, R)] = out.reshape(R, PAIR, piece)

        def send(j, inner):
            there = t * R + j
            d = lax.rem(there - me + E, E)

            @pl.when(d != 0)
            def _():
                back_copy(d, there, me).start()

            return inner

        lax.fori_loop(0, R, send, 0)
        return carry

    lax.fori_loop(0, G, give_back, 0)
    back_r[me] = back_s[me]

    def back_recv(d, carry):
        back_copy(d, me, lax.rem(me - d + E, E)).wait_recv()
        return carry

    lax.fori_loop(1, E, back_recv, 0)
    weights = comb_ref[...]
    high = weights.astype(BF)
    low = (weights - high.astype(F32)).astype(BF)
    returned = back_r[...].reshape(E * PAIR, piece)
    mixed = jnp.dot(high, returned, preferred_element_type=F32) + jnp.dot(
        low, returned, preferred_element_type=F32
    )
    few = mix_ref.shape[0]
    for c in range(CHUNKS):
        mix_ref[:, c * piece : (c + 1) * piece] = mixed[c * few : (c + 1) * few].astype(BF)

    def rep_sent(d, carry):
        attn_copy(d, rep).wait_send()
        cols_copy(d, lax.rem(rep + d, R), rep).wait_send()
        return carry

    lax.fori_loop(1, R, rep_sent, 0)
    for d in range(1, G):
        proj_copy(d).wait_send()

    def pair_sent(d, carry):
        there = lax.rem(me + d, E)
        disp_copy(d, there, me).wait_send()
        back_copy(d, there, me).wait_send()
        return carry

    lax.fori_loop(1, E, pair_sent, 0)
    for i in range(G):
        rows_copy(i, lax.rem(grp + i, G)).wait_send()
    for n in range(CHUNKS):
        half_copy(n).wait_send()


def per_device(
    G, R,
    queries, keys, values, hidden_in, o_weight, norm_gain, routes, route_weights,
    w_gate, w_up, w_down,
):
    E = G * R
    rows_all, width = queries.shape
    span = keys.shape[0]
    few, model = hidden_in.shape
    block = o_weight.shape[1]
    hidden = w_gate.shape[2]
    heads = width // HEAD_DIM
    share = rows_all // R
    lanes = share * heads
    piece = model // CHUNKS
    tall = rows_all // G
    side = E * SLOTS

    hits = (routes[:, :, None] == jnp.arange(E, dtype=jnp.int32)).astype(F32)
    named = jnp.sum(hits, axis=1)
    weight = jnp.sum(hits * route_weights[:, :, None], axis=1)
    before = jnp.stack(
        [jnp.sum(named[:r], axis=0) if r else jnp.zeros_like(named[0]) for r in range(few)]
    )
    slot = jnp.arange(SLOTS, dtype=F32)[None, None, :]
    taken = jnp.where(before[:, :, None] == slot, named[:, :, None], 0.0)
    same = jnp.eye(CHUNKS, dtype=F32)
    sel = (
        jnp.transpose(taken, (1, 2, 0))[:, None, :, None, :] * same[None, :, None, :, None]
    ).reshape(E * PAIR, CHUNKS * few)
    comb = (
        (taken * weight[:, :, None])[None, :, :, None, :] * same[:, None, None, :, None]
    ).reshape(CHUNKS * few, E * PAIR)

    vmem = pl.BlockSpec(memory_space=pltpu.VMEM)
    anywhere = pl.BlockSpec(memory_space=pl.ANY)
    dma = pltpu.SemaphoreType.DMA
    scratch = [
        pltpu.VMEM(queries.shape, BF),
        pltpu.VMEM(keys.shape, BF),
        pltpu.VMEM(values.shape, BF),
        pltpu.VMEM((HEAD_DIM, span), BF),
        pltpu.VMEM(o_weight.shape, BF),
        pltpu.VMEM(w_gate.shape, BF),
        pltpu.VMEM(w_up.shape, BF),
        pltpu.VMEM(w_down.shape, BF),
        dma((7,)),
        pltpu.VMEM((R, HEAD_DIM, lanes), BF),
        pltpu.VMEM((R, 8, lanes), F32),
        pltpu.VMEM((R - 1, HEAD_DIM, lanes), BF),
        pltpu.VMEM((R - 1, 8, lanes), F32),
        pltpu.VMEM((rows_all, width), BF),
        pltpu.VMEM((rows_all, block), F32),
        pltpu.VMEM((G, tall, block), BF),
        pltpu.VMEM((G - 1, tall, block), BF),
        pltpu.VMEM((R, few, block), F32),
        pltpu.VMEM((R, few, block), F32),
        pltpu.VMEM((E, PAIR, piece), BF),
        pltpu.VMEM((E, PAIR, piece), BF),
        pltpu.VMEM((2 * side, model), BF),
        pltpu.VMEM((2 * side, hidden), BF),
        pltpu.VMEM((CHUNKS, 2, side, piece), BF),
        pltpu.VMEM((CHUNKS, side, piece), BF),
        pltpu.VMEM((CHUNKS, side, piece), BF),
        pltpu.VMEM((E, PAIR, piece), BF),
        pltpu.VMEM((E, PAIR, piece), BF),
    ]
    for count in (R - 1, R - 1, R - 1, G - 1, R - 1, E - 1, G, CHUNKS, E - 1):
        scratch += [dma((count,)), dma((count,))]
    return pl.pallas_call(
        functools.partial(layer, G, R),
        out_shape=[jax.ShapeDtypeStruct(hidden_in.shape, BF)] * 2,
        in_specs=[anywhere] * 4 + [vmem] * 4 + [anywhere] * 3,
        out_specs=[vmem] * 2,
        scratch_shapes=scratch,
        compiler_params=pltpu.CompilerParams(
            collective_id=0, has_side_effects=True, vmem_limit_bytes=58 << 20
        ),
        name="decode_layer",
    )(
        queries, keys, values, o_weight,
        hidden_in, norm_gain.reshape(1, model), sel.astype(BF), comb,
        w_gate, w_up, w_down,
    )


def solution(mesh):
    rows = P(("pool", "grp", "rep"), None)
    return jax.shard_map(
        functools.partial(per_device, mesh.shape["grp"], mesh.shape["rep"]),
        mesh=mesh,
        in_specs=(
            P("pool", "grp"),
            P("rep", "grp"),
            P("rep", "grp"),
            rows,
            P("grp", "rep"),
            P(),
            rows,
            rows,
            P(("grp", "rep"), None, "pool"),
            P(("grp", "rep"), None, "pool"),
            P(("grp", "rep"), "pool", None),
        ),
        out_specs=(rows, rows),
        check_vma=False,
    )
```

time: 257 us -> 121 us (0.47)
  waiting for transfers between devices: 114 us -> 0 us
  Pallas kernels: 0 us -> 105 us
  blocking collectives: 55.1 us -> 0 us
  matrix products: 34.3 us -> 0 us
  starting transfers between devices: 17.2 us -> 0 us
  between operations: 14 us -> 0.69 us
  other arithmetic: 9.24 us -> 4.23 us
    pallas_call x0 -> x1, Pallas kernels: none -> 105 us  [per_device(): pl.pallas_call(functools.partial(layer, G, R), out_shape=[jax.ShapeDtypeS...]
    all_gather x2 -> x0, waiting for transfers between devices: 55.1 us -> none  [the longest x1 40.8 us: per_device(): lax.all_gather(attention.reshape(share, heads_local * HEAD_DIM), 'rep', a...]
    all_to_all x2 -> x0, blocking collectives: 55.1 us -> none  [the longest x1 36.5 us: per_device(): lax.all_to_all(payload, 'rep', split_axis=0, concat_axis=0, tiled=True)]
    reduce_scatter x2 -> x0, waiting for transfers between devices: 35.1 us -> none  [the longest x1 18.9 us: per_device(): lax.psum_scatter(jnp.dot(attention, o_weight, preferred_element_type=jnp....]
    dot_general x12 -> x0, matrix products: 34.3 us -> none  [the longest x1 11.3 us: expert_apply(): return jnp.dot(activated, down_w, preferred_element_type=jnp.float32)]
    all_to_all x2 -> x0, waiting for transfers between devices: 23.7 us -> none  [the longest x1 17.4 us: per_device(): lax.all_to_all(served, ('grp', 'rep'), split_axis=0, concat_axis=0, tiled...]
    all_to_all x2 -> x0, starting transfers between devices: 16.8 us -> none  [the longest x1 10.1 us: per_device(): lax.all_to_all(served, ('grp', 'rep'), split_axis=0, concat_axis=0, tiled...]
    reduce_sum x9 -> x3, other arithmetic: 5.63 us -> 0.82 us  [the longest x1 0.79 us: per_device(): weight = jnp.sum(hits * route_weights[:, :, None], axis=1)]
  transfers between devices with their start and end apart: 6 -> 0, of which waited for: 6 -> 0; matrix products, arithmetic and copies ran while one was open for 0% -> 0% of each run, Pallas kernels for 0% -> 0%
where the time goes in v2:
time: 121 us; the launch traced here: 120 us
  Pallas kernels  105 us (87%)
  local copies, waits for them, and re-layouts  10.1 us (8%)
  other arithmetic  4.23 us (3%)
    pallas_call x1, Pallas kernels, per_device(): pl.pallas_call(functools.partial(layer, G, R), out_shape=[jax.ShapeDtypeS...  105 us
    mul x2, local copies, waits for them, and re-layouts, per_device(): (taken * weight[:, :, None])[None, :, :, None, :]  4.09 us
    unnamed x4, local copies, waits for them, and re-layouts  2.77 us
    mul x1, other arithmetic, per_device(): (taken * weight[:, :, None])[None, :, :, None, :]  2.53 us

profile of v2, /device:TPU:1, one launch (start us, length us, event | category | flops | bytes accessed | tf_op | source)
XLA Modules:
  0.0 119.9 jit_solution(7673655697300005735)
XLA Ops:
  0.6 0.8 select_reduce_fusion
  1.5 0.1 pad_maximum_fusion
  1.5 0.1 copy.24
  1.6 0.1 copy.25
  1.7 0.1 copy.26
  1.8 0.1 fusion
  1.9 2.5 %broadcast_multiply_fusion = f32[8,4,64,8,2]{1,0,4,3,2:T(8,128)} fusion(f32[8,8]{0,1:T(8,128)S(1)} %fusion.1, f32[4,64,2]{0,2,1:T(2,128)S(1)} %fusion), kind=kLoop, calls=%fused_computation.1 | loop fusion | flops 32768 | bytes 133376 | tf_op jit(solution)/shard_map/mul | solution.py:417
  4.4 0.0 copy-start
  4.4 3.3 %mul.62 = f32[32,1024]{0,1:T(8,128)S(1)} reshape(f32[8,4,64,8,2]{1,0,4,3,2:T(8,128)} %broadcast_multiply_fusion) | data formatting | bytes 262144 | tf_op jit(solution)/shard_map/mul | solution.py:417
  7.7 0.8 copy.27.comb_ref
  8.5 0.1 fusion.2
  8.6 0.1 copy.21
  8.7 0.1 copy.22
  8.9 0.1 copy.23
  8.9 0.6 multiply_convert_fusion
  9.6 2.1 %convert_element_type.24.sel_ref = bf16[1024,32]{1,0:T(8,128)(2,1)} reshape(bf16[64,8,2,8,4]{4,3,2,1,0:T(8,128)(2,1)S(1)} %multiply_convert_fusion) | data formatting | bytes 131072 | tf_op jit(solution)/shard_map/convert_element_type | solution.py:467
  11.6 0.0 copy-done
  11.6 0.6 reshape.52.gain_ref
  12.2 104.9 %decode_layer.1 = (bf16[4,4096]{1,0:T(4,128)(2,1)}, bf16[4,4096]{1,0:T(4,128)(2,1)}) custom-call(bf16[256,2048]{1,0:T(8,128)(2,1)} %q_hbm.1, bf16[1024,128]{1,0:T(8,128)(2,1)} %k_hbm.1, bf16[1024,128]{1,0:T(8,128)(2,1)} %v_hbm.1, bf16[2048,256]{1,0:T(8,128)(2,1)} %ow_hbm.1, bf16[4,4096]{1,0:T(4,128)(2,1)} %hidden_ref.1, bf16[1,4096]{1,0:T(2,128)(2,1)} %reshape.52.gain_ref, ...), custom_call_target="tpu_custom_call" | custom-call | tf_op jit(solution)/shard_map/decode_layer/pallas_call | solution.py:455
  117.1 1.4 %copy.30 = bf16[4,4096]{1,0:T(4,128)(2,1)} copy(bf16[4,4096]{1,0:T(4,128)(2,1)} %get-tuple-element.6) | data formatting | bytes 65536
  118.5 1.4 %copy.31 = bf16[4,4096]{1,0:T(4,128)(2,1)} copy(bf16[4,4096]{1,0:T(4,128)(2,1)} %get-tuple-element.7) | data formatting | bytes 65536
  (6 shorter events, 0.1 us)
Async XLA Ops:
  4.4 7.2 %copy-start = (bf16[4096]{0:T(1024)(128)(2,1)S(1)}, bf16[4096]{0:T(1024)(128)(2,1)}, u32[]{:S(2)}) copy-start(bf16[4096]{0:T(1024)(128)(2,1)} %param.16) | copy-start | bytes 24580

commit v3 on v2

v3 whole, which is shorter than its diff:
```python
import functools
import math

import jax
import jax.numpy as jnp
from jax import lax
from jax.experimental import pallas as pl
from jax.experimental.pallas import tpu as pltpu
from jax.sharding import PartitionSpec as P

HEAD_DIM = 128
CHUNKS = 8
SLOTS = 2
PAIR = CHUNKS * SLOTS
MESH = pl.DeviceIdType.MESH
BF = jnp.bfloat16
F32 = jnp.float32


def remote(src, dst, send, recv, where):
    return pltpu.make_async_remote_copy(
        src_ref=src,
        dst_ref=dst,
        send_sem=send,
        recv_sem=recv,
        device_id=where,
        device_id_type=MESH,
    )


def layer(
    G, R,
    q_hbm, k_hbm, v_hbm, ow_hbm, hidden_ref, gain_ref, routes_ref, weights_ref, wg_hbm, wu_hbm, wd_hbm,
    mid_ref, mix_ref,
    q_s, k_s, v_s, ow_s, wg_s, wu_s, wd_s, load_sem,
    part_s, stat_s, part_r, stat_r, attn_s,
    cols_s, cols_r, sel_s, comb_s,
    disp_s, disp_r, rows_s, act_s, half_s, half_r, sum_s, back_s, back_r,
    part_ss, part_rs, stat_ss, stat_rs, attn_ss, attn_rs,
    cols_ss, cols_rs, disp_ss, disp_rs,
    rows_ss, rows_rs, half_ss, half_rs, back_ss, back_rs,
):
    pool, grp, rep = lax.axis_index("pool"), lax.axis_index("grp"), lax.axis_index("rep")
    E = G * R
    wide = math.isqrt(R)
    me = grp * R + rep
    sibling = (1 - pool, grp, rep)

    way = 1 - 2 * pool
    x, z = rep // wide, rep % wide
    ahead_y = [lax.rem(grp + way * d + G, G) for d in range(G)]
    behind_y = [lax.rem(grp - way * d + G, G) for d in range(G)]
    ahead_x = [lax.rem(x + way * d + wide, wide) * wide for d in range(wide)]
    behind_x = [lax.rem(x - way * d + wide, wide) * wide for d in range(wide)]
    ahead_z = [lax.rem(z + way * d + wide, wide) for d in range(wide)]
    behind_z = [lax.rem(z - way * d + wide, wide) for d in range(wide)]

    def ahead(d):
        d, plane = d % R, d // R
        return ahead_y[plane], ahead_x[d // wide] + ahead_z[d % wide]

    def behind(d):
        d, plane = d % R, d // R
        return behind_y[plane], behind_x[d // wide] + behind_z[d % wide]

    near = [i * (R // 2 - 1) % R for i in range(1, R)]
    far = [i * (E // 2 - 5) % E for i in range(1, E)]

    loads = [
        pltpu.make_async_copy(src, dst, load_sem.at[i])
        for i, (src, dst) in enumerate(
            (
                (q_hbm, q_s),
                (k_hbm, k_s),
                (v_hbm, v_s),
                (ow_hbm, ow_s),
                (wg_hbm, wg_s),
                (wu_hbm, wu_s),
                (wd_hbm, wd_s),
            )
        )
    ]
    for load in loads[:3]:
        load.start()

    barrier = pltpu.get_barrier_semaphore()
    for d in far:
        pl.semaphore_signal(barrier, inc=1, device_id=(pool, *ahead(d)), device_id_type=MESH)
    pl.semaphore_signal(barrier, inc=1, device_id=sibling, device_id_type=MESH)

    lane = lax.broadcasted_iota(jnp.int32, (1, E * PAIR), 1)
    expert, chunk, slot = lane // PAIR, lane % PAIR // SLOTS, lane % SLOTS
    few, topk = routes_ref.shape
    before = jnp.zeros((1, E * PAIR), jnp.int32)
    taken, weights = [], []
    for r in range(few):
        named, weight = jnp.zeros_like(before), jnp.zeros(before.shape, F32)
        for k in range(topk):
            hit = expert == routes_ref[r, k]
            named = jnp.where(hit, 1, named)
            weight = jnp.where(hit, weights_ref[r, k], weight)
        use = jnp.where(before == slot, named, 0).astype(F32)
        taken.append(use)
        weights.append(use * weight)
        before = before + named
    of_row = lax.broadcasted_iota(jnp.int32, (CHUNKS * few, E * PAIR), 0) // few
    select = jnp.where(of_row == chunk, jnp.concatenate(taken * CHUNKS, axis=0), 0.0)
    sel_s[...] = select.T.astype(BF)
    combine = jnp.where(of_row == chunk, jnp.concatenate(weights * CHUNKS, axis=0), 0.0)
    high = combine.astype(BF)
    comb_s[0] = high
    comb_s[1] = (combine - high.astype(F32)).astype(BF)

    for load in loads[:3]:
        load.wait()
    for load in loads[3:]:
        load.start()
    pl.semaphore_wait(barrier, E)

    rows_all, width = q_s.shape
    heads = width // HEAD_DIM
    share = rows_all // R
    lanes = share * heads
    scale = HEAD_DIM ** (-0.5)
    order = R // 2 - 1

    def target(s):
        d = lax.rem((s + 1) * order, R)
        across = lax.rem(x + way * (d // wide) + wide, wide)
        return across * wide + lax.rem(z + way * lax.rem(d, wide) + wide, wide)

    def part_copy(s, peer):
        where = (pool, grp, peer)
        return (
            remote(part_s.at[s], part_r.at[s], part_ss.at[s], part_rs.at[s], where),
            remote(stat_s.at[s], stat_r.at[s], stat_ss.at[s], stat_rs.at[s], where),
        )

    def attend(s):
        peer = target(s)
        block = pl.ds(pl.multiple_of(peer * share, share), share)
        query = jnp.concatenate(
            [q_s[block, h * HEAD_DIM : (h + 1) * HEAD_DIM] for h in range(heads)], axis=0
        )
        scores = lax.dot_general(
            query, k_s[...], (((1,), (1,)), ((), ())), preferred_element_type=F32
        )
        top = jnp.max(scores, axis=1, keepdims=True)
        probs = jnp.exp((scores - top) * scale)
        total = jnp.sum(probs, axis=1, keepdims=True)
        part = jnp.dot(probs.astype(BF), v_s[...], preferred_element_type=F32)
        part_s[s] = part.astype(BF)
        first = lax.broadcasted_iota(jnp.int32, (lanes, 128), 1) < 4
        stat_s[s] = jnp.where(first, top, total).T[:8]

        @pl.when(s < R - 1)
        def _():
            for copy in part_copy(s, peer):
                copy.start()

    unroll = 4

    def attend_some(i, carry):
        for j in range(unroll):
            attend(i * unroll + j)
        return carry

    lax.fori_loop(0, R // unroll, attend_some, 0)
    for s in range(R - 1):
        for copy in part_copy(s, rep):
            copy.wait_recv()

    stats = [stat_r[s] for s in range(R - 1)] + [stat_s[R - 1]]
    top = functools.reduce(jnp.maximum, [stat[0:1] for stat in stats])
    factors = [jnp.exp((stat[0:1] - top) * scale) for stat in stats]
    total = functools.reduce(
        jnp.add, [stat[4:5] * factor for stat, factor in zip(stats, factors)]
    )
    factors = [factor / total for factor in factors]
    factors = jnp.concatenate(factors + [jnp.zeros((128 - R, lanes), F32)], axis=0).T
    weighted = part_s[R - 1].astype(F32) * factors[:, R - 1 : R]
    for s in range(R - 1):
        weighted += part_r[s].astype(F32) * factors[:, s : s + 1]
    attention = weighted.astype(BF)
    mine = pl.ds(pl.multiple_of(rep * share, share), share)
    for h in range(heads):
        attn_s[mine, h * HEAD_DIM : (h + 1) * HEAD_DIM] = attention[h * share : (h + 1) * share]

    def attn_copy(d, block):
        at = attn_s.at[pl.ds(pl.multiple_of(block * share, share), share)]
        return remote(at, at, attn_ss.at[d - 1], attn_rs.at[d - 1], (pool, *ahead(d)))

    for d in near:
        attn_copy(d, rep).start()
    for d in near:
        attn_copy(d, behind(d)[1]).wait_recv()
    loads[3].wait()
    projected = jnp.dot(attn_s[...], ow_s[...], preferred_element_type=F32)
    for e in range(E):
        cols_s[e] = projected[e * few : (e + 1) * few]

    def pair_copy(src, dst, send, recv, d, a, b):
        return remote(
            src.at[a], dst.at[b], send.at[d - 1], recv.at[d - 1], (pool, *ahead(d))
        )

    def cols_copy(d, a, b):
        return pair_copy(cols_s, cols_r, cols_ss, cols_rs, d, a, b)

    def disp_copy(d, a, b):
        return pair_copy(disp_s, disp_r, disp_ss, disp_rs, d, a, b)

    def back_copy(d, a, b):
        return pair_copy(back_s, back_r, back_ss, back_rs, d, a, b)

    def to(d):
        there, along = ahead(d)
        return there * R + along

    def source(d):
        there, along = behind(d)
        return there * R + along

    for d in far:
        cols_copy(d, to(d), me).start()
    cols_r[me] = cols_s[me]
    for d in far:
        cols_copy(d, me, source(d)).wait_recv()
    summed = cols_r[0:R]
    for g in range(1, G):
        summed = summed + cols_r[g * R : (g + 1) * R]
    summed = summed.astype(BF).astype(F32)
    projected = jnp.concatenate([summed[j] for j in range(R)], axis=1)
    mid = (hidden_ref[...].astype(F32) + projected).astype(BF)
    mid_ref[...] = mid
    wider = mid.astype(F32)
    inverse = lax.rsqrt(jnp.mean(wider * wider, axis=-1, keepdims=True) + 1e-06)
    normed = wider * inverse * gain_ref[...].astype(F32).reshape(1, -1)
    piece = normed.shape[1] // CHUNKS
    pieces = jnp.concatenate(
        [normed[:, c * piece : (c + 1) * piece] for c in range(CHUNKS)], axis=0
    ).astype(BF)

    tile = R * PAIR
    for t in range(G):
        chosen = jnp.dot(
            sel_s[t * tile : (t + 1) * tile, :], pieces, preferred_element_type=F32
        )
        disp_s[t * R : (t + 1) * R] = chosen.astype(BF).reshape(R, PAIR, piece)
    for d in far:
        disp_copy(d, to(d), me).start()
    disp_r[me] = disp_s[me]

    row = lax.broadcasted_iota(jnp.int32, (tile, tile), 0)
    col = lax.broadcasted_iota(jnp.int32, (tile, tile), 1)
    pairs = R * SLOTS

    def moved(i):
        return lax.rem(i, pairs) // SLOTS * PAIR + i // pairs * SLOTS + lax.rem(i, SLOTS)

    gather = jnp.where(col == moved(row), 1.0, 0.0).astype(BF)
    spread = jnp.where(row == moved(col), 1.0, 0.0).astype(BF)
    side = E * SLOTS

    def rows_copy(i, half, t):
        at = rows_s.at[pl.ds(pl.multiple_of(half * side + t * pairs, pairs), pairs)]
        return remote(at, at, rows_ss.at[i], rows_rs.at[i], sibling)

    for i in range(G):
        t = behind_y[i]
        for d in range(i * R, (i + 1) * R):
            if d:
                disp_copy(d, me, source(d)).wait_recv()
        arrived = disp_r[pl.ds(t * R, R)].reshape(tile, piece)
        ordered = jnp.dot(gather, arrived, preferred_element_type=F32).astype(BF)
        at = pl.ds(pl.multiple_of(pool * side + t * pairs, pairs), pairs)
        for c in range(CHUNKS):
            rows_s[at, c * piece : (c + 1) * piece] = ordered[c * pairs : (c + 1) * pairs]
        rows_copy(i, pool, t).start()
    for i in range(G):
        rows_copy(i, 1 - pool, ahead_y[i]).wait_recv()
    loads[4].wait()
    loads[5].wait()
    hidden = act_s.shape[1]
    step = min(256, hidden)

    def expand(n, carry):
        at = pl.ds(pl.multiple_of(n * step, step), step)
        gate = jnp.dot(rows_s[...], wg_s[0, :, at], preferred_element_type=F32)
        upper = jnp.dot(rows_s[...], wu_s[0, :, at], preferred_element_type=F32)
        act_s[:, at] = (gate / (1.0 + jnp.exp(-gate)) * upper).astype(BF)
        return carry

    lax.fori_loop(0, hidden // step, expand, 0)
    loads[6].wait()

    def half_copy(n):
        return remote(
            half_s.at[n, 1 - pool], half_r.at[n], half_ss.at[n], half_rs.at[n], sibling
        )

    def contract(n, carry):
        at = pl.ds(pl.multiple_of(n * piece, piece), piece)
        out = jnp.dot(act_s[...], wd_s[0, :, at], preferred_element_type=F32)
        half_s[n, 0] = out[:side].astype(BF)
        half_s[n, 1] = out[side:].astype(BF)
        half_copy(n).start()
        return carry

    lax.fori_loop(0, CHUNKS, contract, 0)
    for n in range(CHUNKS):
        half_copy(n).wait_recv()
        sum_s[n] = (half_s[n, pool].astype(F32) + half_r[n].astype(F32)).astype(BF)
    for t in range(G):
        stacked = sum_s[:, t * pairs : (t + 1) * pairs, :].reshape(tile, piece)
        out = jnp.dot(spread, stacked, preferred_element_type=F32).astype(BF)
        back_s[t * R : (t + 1) * R] = out.reshape(R, PAIR, piece)
    for d in far:
        back_copy(d, to(d), me).start()
    back_r[me] = back_s[me]
    for d in far:
        back_copy(d, me, source(d)).wait_recv()
    returned = back_r[...].reshape(E * PAIR, piece)
    mixed = jnp.dot(comb_s[0], returned, preferred_element_type=F32) + jnp.dot(
        comb_s[1], returned, preferred_element_type=F32
    )
    for c in range(CHUNKS):
        mix_ref[:, c * piece : (c + 1) * piece] = mixed[c * few : (c + 1) * few].astype(BF)

    for s in range(R - 1):
        for copy in part_copy(s, rep):
            copy.wait_send()
    for d in near:
        attn_copy(d, rep).wait_send()
    for d in far:
        cols_copy(d, to(d), me).wait_send()
        disp_copy(d, to(d), me).wait_send()
        back_copy(d, to(d), me).wait_send()
    for i in range(G):
        rows_copy(i, pool, behind_y[i]).wait_send()
    for n in range(CHUNKS):
        half_copy(n).wait_send()


def per_device(
    G, R,
    queries, keys, values, hidden_in, o_weight, norm_gain, routes, route_weights,
    w_gate, w_up, w_down,
):
    E = G * R
    rows_all, width = queries.shape
    few, model = hidden_in.shape
    block = o_weight.shape[1]
    hidden = w_gate.shape[2]
    heads = width // HEAD_DIM
    share = rows_all // R
    lanes = share * heads
    piece = model // CHUNKS
    side = E * SLOTS

    vmem = pl.BlockSpec(memory_space=pltpu.VMEM)
    smem = pl.BlockSpec(memory_space=pltpu.SMEM)
    anywhere = pl.BlockSpec(memory_space=pl.ANY)
    dma = pltpu.SemaphoreType.DMA
    scratch = [
        pltpu.VMEM(queries.shape, BF),
        pltpu.VMEM(keys.shape, BF),
        pltpu.VMEM(values.shape, BF),
        pltpu.VMEM(o_weight.shape, BF),
        pltpu.VMEM(w_gate.shape, BF),
        pltpu.VMEM(w_up.shape, BF),
        pltpu.VMEM(w_down.shape, BF),
        dma((7,)),
        pltpu.VMEM((R, lanes, HEAD_DIM), BF),
        pltpu.VMEM((R, 8, lanes), F32),
        pltpu.VMEM((R - 1, lanes, HEAD_DIM), BF),
        pltpu.VMEM((R - 1, 8, lanes), F32),
        pltpu.VMEM((rows_all, width), BF),
        pltpu.VMEM((E, few, block), F32),
        pltpu.VMEM((E, few, block), F32),
        pltpu.VMEM((E * PAIR, CHUNKS * few), BF),
        pltpu.VMEM((2, CHUNKS * few, E * PAIR), BF),
        pltpu.VMEM((E, PAIR, piece), BF),
        pltpu.VMEM((E, PAIR, piece), BF),
        pltpu.VMEM((2 * side, model), BF),
        pltpu.VMEM((2 * side, hidden), BF),
        pltpu.VMEM((CHUNKS, 2, side, piece), BF),
        pltpu.VMEM((CHUNKS, side, piece), BF),
        pltpu.VMEM((CHUNKS, side, piece), BF),
        pltpu.VMEM((E, PAIR, piece), BF),
        pltpu.VMEM((E, PAIR, piece), BF),
    ]
    for count in (R - 1, R - 1, R - 1, E - 1, E - 1, G, CHUNKS, E - 1):
        scratch += [dma((count,)), dma((count,))]
    return pl.pallas_call(
        functools.partial(layer, G, R),
        out_shape=[jax.ShapeDtypeStruct(hidden_in.shape, BF)] * 2,
        in_specs=[anywhere] * 4 + [vmem] * 2 + [smem] * 2 + [anywhere] * 3,
        out_specs=[vmem] * 2,
        scratch_shapes=scratch,
        compiler_params=pltpu.CompilerParams(
            collective_id=0, has_side_effects=True, vmem_limit_bytes=58 << 20
        ),
        name="decode_layer",
    )(
        queries, keys, values, o_weight,
        hidden_in, norm_gain, routes, route_weights,
        w_gate, w_up, w_down,
    )


def solution(mesh):
    rows = P(("pool", "grp", "rep"), None)
    return jax.shard_map(
        functools.partial(per_device, mesh.shape["grp"], mesh.shape["rep"]),
        mesh=mesh,
        in_specs=(
            P("pool", "grp"),
            P("rep", "grp"),
            P("rep", "grp"),
            rows,
            P("grp", "rep"),
            P(),
            rows,
            rows,
            P(("grp", "rep"), None, "pool"),
            P(("grp", "rep"), None, "pool"),
            P(("grp", "rep"), "pool", None),
        ),
        out_specs=(rows, rows),
        check_vma=False,
    )
```

time: 121 us -> 102 us (0.84)
  local copies, waits for them, and re-layouts: 10.1 us -> 2.77 us
  Pallas kernels: 105 us -> 97.7 us
  other arithmetic: 4.23 us -> 0 us
    pallas_call x1, Pallas kernels: 105 us -> 97.7 us  [per_device(): pl.pallas_call(functools.partial(layer, G, R), out_shape=[jax.ShapeDtypeS...]
    mul x2 -> x0, local copies, waits for them, and re-layouts: 4.09 us -> none  [per_device(): (taken * weight[:, :, None])[None, :, :, None, :]]
    mul x2 -> x0, other arithmetic: 2.58 us -> none  [the longest x1 2.53 us: per_device(): (taken * weight[:, :, None])[None, :, :, None, :]]
    convert_element_type x2 -> x0, local copies, waits for them, and re-layouts: 2.13 us -> none  [the longest x1 2.06 us: per_device(): sel.astype(BF)]
    unnamed x4 -> x2, local copies, waits for them, and re-layouts: 2.77 us -> 2.77 us
where the time goes in v3:
time: 102 us; the launch traced here: 101 us
  Pallas kernels  97.7 us (96%)
  local copies, waits for them, and re-layouts  2.77 us (3%)
    pallas_call x1, Pallas kernels, per_device(): pl.pallas_call(functools.partial(layer, G, R), out_shape=[jax.ShapeDtypeS...  97.7 us
    unnamed x2, local copies, waits for them, and re-layouts  2.77 us

profile of v3, /device:TPU:1, one launch (start us, length us, event | category | flops | bytes accessed | tf_op | source)
XLA Modules:
  0.0 101.1 jit_solution(18106626597579802398)
XLA Ops:
  0.6 97.7 %decode_layer.1 = (bf16[4,4096]{1,0:T(4,128)(2,1)}, bf16[4,4096]{1,0:T(4,128)(2,1)}) custom-call(bf16[256,2048]{1,0:T(8,128)(2,1)} %q_hbm.1, bf16[1024,128]{1,0:T(8,128)(2,1)} %k_hbm.1, bf16[1024,128]{1,0:T(8,128)(2,1)} %v_hbm.1, bf16[2048,256]{1,0:T(8,128)(2,1)} %ow_hbm.1, bf16[4,4096]{1,0:T(4,128)(2,1)} %hidden_ref.1, bf16[4096]{0:T(1024)(128)(2,1)} %gain_ref.1, ...), custom_call_target="tpu_custom_call" | custom-call | tf_op jit(solution)/shard_map/decode_layer/pallas_call | solution.py:395
  98.4 1.4 %copy.15 = bf16[4,4096]{1,0:T(4,128)(2,1)} copy(bf16[4,4096]{1,0:T(4,128)(2,1)} %get-tuple-element.4) | data formatting | bytes 65536
  99.7 1.4 %copy.16 = bf16[4,4096]{1,0:T(4,128)(2,1)} copy(bf16[4,4096]{1,0:T(4,128)(2,1)} %get-tuple-element.5) | data formatting | bytes 65536

commit v4 on v3

--- a/solution.py
+++ b/solution.py
@@ -34,7 +34,7 @@
     mid_ref, mix_ref,
     q_s, k_s, v_s, ow_s, wg_s, wu_s, wd_s, load_sem,
     part_s, stat_s, part_r, stat_r, attn_s,
-    cols_s, cols_r, sel_s, comb_s,
+    cols_s, cols_r, sel_s, comb_s, perm_s,
     disp_s, disp_r, rows_s, act_s, half_s, half_r, sum_s, back_s, back_r,
     part_ss, part_rs, stat_ss, stat_rs, attn_ss, attn_rs,
     cols_ss, cols_rs, disp_ss, disp_rs,
@@ -88,9 +88,99 @@
         pl.semaphore_signal(barrier, inc=1, device_id=(pool, *ahead(d)), device_id_type=MESH)
     pl.semaphore_signal(barrier, inc=1, device_id=sibling, device_id_type=MESH)
 
+    for load in loads[:3]:
+        load.wait()
+    loads[3].start()
+
+    rows_all, width = q_s.shape
+    heads = width // HEAD_DIM
+    share = rows_all // R
+    lanes = share * heads
+    scale = HEAD_DIM ** (-0.5)
+    order = R // 2 - 1
+
+    def target(s):
+        d = lax.rem((s + 1) * order, R)
+        across = lax.rem(x + way * (d // wide) + wide, wide)
+        return across * wide + lax.rem(z + way * lax.rem(d, wide) + wide, wide)
+
+    def part_copy(s, peer):
+        where = (pool, grp, peer)
+        return (
+            remote(part_s.at[s], part_r.at[s], part_ss.at[s], part_rs.at[s], where),
+            remote(stat_s.at[s], stat_r.at[s], stat_ss.at[s], stat_rs.at[s], where),
+        )
+
+    def attend(s):
+        peer = target(s)
+        block = pl.ds(pl.multiple_of(peer * share, share), share)
+        query = jnp.concatenate(
+            [q_s[block, h * HEAD_DIM : (h + 1) * HEAD_DIM] for h in range(heads)], axis=0
+        )
+        scores = lax.dot_general(
+            query, k_s[...], (((1,), (1,)), ((), ())), preferred_element_type=F32
+        )
+        top = jnp.max(scores, axis=1, keepdims=True)
+        probs = jnp.exp((scores - top) * scale)
+        total = jnp.sum(probs, axis=1, keepdims=True)
+        part = jnp.dot(probs.astype(BF), v_s[...], preferred_element_type=F32)
+        part_s[s] = part.astype(BF)
+        first = lax.broadcasted_iota(jnp.int32, (lanes, 128), 1) < 4
+        stat_s[s] = jnp.where(first, top, total).T[:8]
+
+    unroll = 4
+
+    def attend_some(i, carry):
+        for j in range(unroll):
+            s = i * unroll + j
+            attend(s)
+
+            @pl.when(s < R - 1)
+            def _():
+                for copy in part_copy(s, target(s)):
+                    copy.start()
+
+        return carry
+
+    few, topk = routes_ref.shape
+    for s in range(unroll):
+        attend(s)
+    pl.semaphore_wait(barrier, E)
+    for s in range(min(unroll, R - 1)):
+        for copy in part_copy(s, target(s)):
+            copy.start()
+    lax.fori_loop(1, R // unroll, attend_some, 0)
+    for s in range(R - 1):
+        for copy in part_copy(s, rep):
+            copy.wait_recv()
+
+    stats = [stat_r[s] for s in range(R - 1)] + [stat_s[R - 1]]
+    top = functools.reduce(jnp.maximum, [stat[0:1] for stat in stats])
+    factors = [jnp.exp((stat[0:1] - top) * scale) for stat in stats]
+    total = functools.reduce(
+        jnp.add, [stat[4:5] * factor for stat, factor in zip(stats, factors)]
+    )
+    factors = [factor / total for factor in factors]
+    factors = jnp.concatenate(factors + [jnp.zeros((128 - R, lanes), F32)], axis=0).T
+    weighted = part_s[R - 1].astype(F32) * factors[:, R - 1 : R]
+    for s in range(R - 1):
+        weighted += part_r[s].astype(F32) * factors[:, s : s + 1]
+    attention = weighted.astype(BF)
+    mine = pl.ds(pl.multiple_of(rep * share, share), share)
+    for h in range(heads):
+        attn_s[mine, h * HEAD_DIM : (h + 1) * HEAD_DIM] = attention[h * share : (h + 1) * share]
+
+    def attn_copy(d, block):
+        at = attn_s.at[pl.ds(pl.multiple_of(block * share, share), share)]
+        return remote(at, at, attn_ss.at[d - 1], attn_rs.at[d - 1], (pool, *ahead(d)))
+
+    for d in near:
+        attn_copy(d, rep).start()
+    for load in loads[4:]:
+        load.start()
+
     lane = lax.broadcasted_iota(jnp.int32, (1, E * PAIR), 1)
     expert, chunk, slot = lane // PAIR, lane % PAIR // SLOTS, lane % SLOTS
-    few, topk = routes_ref.shape
     before = jnp.zeros((1, E * PAIR), jnp.int32)
     taken, weights = [], []
     for r in range(few):
@@ -111,87 +201,17 @@
     comb_s[0] = high
     comb_s[1] = (combine - high.astype(F32)).astype(BF)
 
-    for load in loads[:3]:
-        load.wait()
-    for load in loads[3:]:
-        load.start()
-    pl.semaphore_wait(barrier, E)
-
-    rows_all, width = q_s.shape
-    heads = width // HEAD_DIM
-    share = rows_all // R
-    lanes = share * heads
-    scale = HEAD_DIM ** (-0.5)
-    order = R // 2 - 1
-
-    def target(s):
-        d = lax.rem((s + 1) * order, R)
-        across = lax.rem(x + way * (d // wide) + wide, wide)
-        return across * wide + lax.rem(z + way * lax.rem(d, wide) + wide, wide)
-
-    def part_copy(s, peer):
-        where = (pool, grp, peer)
-        return (
-            remote(part_s.at[s], part_r.at[s], part_ss.at[s], part_rs.at[s], where),
-            remote(stat_s.at[s], stat_r.at[s], stat_ss.at[s], stat_rs.at[s], where),
-        )
-
-    def attend(s):
-        peer = target(s)
-        block = pl.ds(pl.multiple_of(peer * share, share), share)
-        query = jnp.concatenate(
-            [q_s[block, h * HEAD_DIM : (h + 1) * HEAD_DIM] for h in range(heads)], axis=0
-        )
-        scores = lax.dot_general(
-            query, k_s[...], (((1,), (1,)), ((), ())), preferred_element_type=F32
-        )
-        top = jnp.max(scores, axis=1, keepdims=True)
-        probs = jnp.exp((scores - top) * scale)
-        total = jnp.sum(probs, axis=1, keepdims=True)
-        part = jnp.dot(probs.astype(BF), v_s[...], preferred_element_type=F32)
-        part_s[s] = part.astype(BF)
-        first = lax.broadcasted_iota(jnp.int32, (lanes, 128), 1) < 4
-        stat_s[s] = jnp.where(first, top, total).T[:8]
-
-        @pl.when(s < R - 1)
-        def _():
-            for copy in part_copy(s, peer):
-                copy.start()
-
-    unroll = 4
-
-    def attend_some(i, carry):
-        for j in range(unroll):
-            attend(i * unroll + j)
-        return carry
-
-    lax.fori_loop(0, R // unroll, attend_some, 0)
-    for s in range(R - 1):
-        for copy in part_copy(s, rep):
-            copy.wait_recv()
-
-    stats = [stat_r[s] for s in range(R - 1)] + [stat_s[R - 1]]
-    top = functools.reduce(jnp.maximum, [stat[0:1] for stat in stats])
-    factors = [jnp.exp((stat[0:1] - top) * scale) for stat in stats]
-    total = functools.reduce(
-        jnp.add, [stat[4:5] * factor for stat, factor in zip(stats, factors)]
-    )
-    factors = [factor / total for factor in factors]
-    factors = jnp.concatenate(factors + [jnp.zeros((128 - R, lanes), F32)], axis=0).T
-    weighted = part_s[R - 1].astype(F32) * factors[:, R - 1 : R]
-    for s in range(R - 1):
-        weighted += part_r[s].astype(F32) * factors[:, s : s + 1]
-    attention = weighted.astype(BF)
-    mine = pl.ds(pl.multiple_of(rep * share, share), share)
-    for h in range(heads):
-        attn_s[mine, h * HEAD_DIM : (h + 1) * HEAD_DIM] = attention[h * share : (h + 1) * share]
-
-    def attn_copy(d, block):
-        at = attn_s.at[pl.ds(pl.multiple_of(block * share, share), share)]
-        return remote(at, at, attn_ss.at[d - 1], attn_rs.at[d - 1], (pool, *ahead(d)))
-
-    for d in near:
-        attn_copy(d, rep).start()
+    tile = R * PAIR
+    pairs = R * SLOTS
+    row = lax.broadcasted_iota(jnp.int32, (tile, tile), 0)
+    col = lax.broadcasted_iota(jnp.int32, (tile, tile), 1)
+
+    def moved(i):
+        return lax.rem(i, pairs) // SLOTS * PAIR + i // pairs * SLOTS + lax.rem(i, SLOTS)
+
+    perm_s[0] = jnp.where(col == moved(row), 1.0, 0.0).astype(BF)
+    perm_s[1] = jnp.where(row == moved(col), 1.0, 0.0).astype(BF)
+
     for d in near:
         attn_copy(d, behind(d)[1]).wait_recv()
     loads[3].wait()
@@ -241,82 +261,96 @@
         [normed[:, c * piece : (c + 1) * piece] for c in range(CHUNKS)], axis=0
     ).astype(BF)
 
-    tile = R * PAIR
-    for t in range(G):
-        chosen = jnp.dot(
-            sel_s[t * tile : (t + 1) * tile, :], pieces, preferred_element_type=F32
-        )
-        disp_s[t * R : (t + 1) * R] = chosen.astype(BF).reshape(R, PAIR, piece)
-    for d in far:
-        disp_copy(d, to(d), me).start()
+    planes = G // 2
+    groups = [range(j * planes, (j + 1) * planes) for j in range(2)]
+
+    def sent(j, sign):
+        return [d for d in far if sign * (d // R) % G in groups[j]]
+
+    for j in range(2):
+        for i in groups[j]:
+            t = ahead_y[i]
+            chosen = jnp.dot(
+                sel_s[pl.ds(pl.multiple_of(t * tile, tile), tile), :],
+                pieces,
+                preferred_element_type=F32,
+            )
+            disp_s[pl.ds(t * R, R)] = chosen.astype(BF).reshape(R, PAIR, piece)
+        for d in sent(j, 1):
+            disp_copy(d, to(d), me).start()
     disp_r[me] = disp_s[me]
-
-    row = lax.broadcasted_iota(jnp.int32, (tile, tile), 0)
-    col = lax.broadcasted_iota(jnp.int32, (tile, tile), 1)
-    pairs = R * SLOTS
-
-    def moved(i):
-        return lax.rem(i, pairs) // SLOTS * PAIR + i // pairs * SLOTS + lax.rem(i, SLOTS)
-
-    gather = jnp.where(col == moved(row), 1.0, 0.0).astype(BF)
-    spread = jnp.where(row == moved(col), 1.0, 0.0).astype(BF)
-    side = E * SLOTS
-
-    def rows_copy(i, half, t):
-        at = rows_s.at[pl.ds(pl.multiple_of(half * side + t * pairs, pairs), pairs)]
+    half = planes * pairs
+
+    def rows_copy(i, of):
+        at = rows_s.at[i // planes, pl.ds(of * half + i % planes * pairs, pairs)]
         return remote(at, at, rows_ss.at[i], rows_rs.at[i], sibling)
 
-    for i in range(G):
-        t = behind_y[i]
-        for d in range(i * R, (i + 1) * R):
-            if d:
-                disp_copy(d, me, source(d)).wait_recv()
-        arrived = disp_r[pl.ds(t * R, R)].reshape(tile, piece)
-        ordered = jnp.dot(gather, arrived, preferred_element_type=F32).astype(BF)
-        at = pl.ds(pl.multiple_of(pool * side + t * pairs, pairs), pairs)
-        for c in range(CHUNKS):
-            rows_s[at, c * piece : (c + 1) * piece] = ordered[c * pairs : (c + 1) * pairs]
-        rows_copy(i, pool, t).start()
-    for i in range(G):
-        rows_copy(i, 1 - pool, ahead_y[i]).wait_recv()
-    loads[4].wait()
-    loads[5].wait()
+    def collect(j):
+        for i in groups[j]:
+            for d in range(i * R, (i + 1) * R):
+                if d:
+                    disp_copy(d, me, source(d)).wait_recv()
+            arrived = disp_r[pl.ds(behind_y[i] * R, R)].reshape(tile, piece)
+            ordered = jnp.dot(perm_s[0], arrived, preferred_element_type=F32).astype(BF)
+            at = pl.ds(pl.multiple_of(pool * half + i % planes * pairs, pairs), pairs)
+            for c in range(CHUNKS):
+                rows_s[j, at, c * piece : (c + 1) * piece] = ordered[c * pairs : (c + 1) * pairs]
+            rows_copy(i, pool).start()
+
     hidden = act_s.shape[1]
     step = min(256, hidden)
 
-    def expand(n, carry):
-        at = pl.ds(pl.multiple_of(n * step, step), step)
-        gate = jnp.dot(rows_s[...], wg_s[0, :, at], preferred_element_type=F32)
-        upper = jnp.dot(rows_s[...], wu_s[0, :, at], preferred_element_type=F32)
-        act_s[:, at] = (gate / (1.0 + jnp.exp(-gate)) * upper).astype(BF)
-        return carry
-
-    lax.fori_loop(0, hidden // step, expand, 0)
-    loads[6].wait()
-
-    def half_copy(n):
+    def half_copy(j, n):
         return remote(
-            half_s.at[n, 1 - pool], half_r.at[n], half_ss.at[n], half_rs.at[n], sibling
-        )
-
-    def contract(n, carry):
-        at = pl.ds(pl.multiple_of(n * piece, piece), piece)
-        out = jnp.dot(act_s[...], wd_s[0, :, at], preferred_element_type=F32)
-        half_s[n, 0] = out[:side].astype(BF)
-        half_s[n, 1] = out[side:].astype(BF)
-        half_copy(n).start()
-        return carry
-
-    lax.fori_loop(0, CHUNKS, contract, 0)
-    for n in range(CHUNKS):
-        half_copy(n).wait_recv()
-        sum_s[n] = (half_s[n, pool].astype(F32) + half_r[n].astype(F32)).astype(BF)
-    for t in range(G):
-        stacked = sum_s[:, t * pairs : (t + 1) * pairs, :].reshape(tile, piece)
-        out = jnp.dot(spread, stacked, preferred_element_type=F32).astype(BF)
-        back_s[t * R : (t + 1) * R] = out.reshape(R, PAIR, piece)
-    for d in far:
-        back_copy(d, to(d), me).start()
+            half_s.at[j, n, 1 - pool], half_r.at[j, n], half_ss.at[j, n], half_rs.at[j, n], sibling
+        )
+
+    def apply(j):
+        for i in groups[j]:
+            rows_copy(i, 1 - pool).wait_recv()
+        if j == 0:
+            loads[4].wait()
+            loads[5].wait()
+
+        def expand(n, carry):
+            at = pl.ds(pl.multiple_of(n * step, step), step)
+            gate = jnp.dot(rows_s[j], wg_s[0, :, at], preferred_element_type=F32)
+            upper = jnp.dot(rows_s[j], wu_s[0, :, at], preferred_element_type=F32)
+            act_s[:, at] = (gate / (1.0 + jnp.exp(-gate)) * upper).astype(BF)
+            return carry
+
+        lax.fori_loop(0, hidden // step, expand, 0)
+        if j == 0:
+            loads[6].wait()
+
+        def contract(n, carry):
+            at = pl.ds(pl.multiple_of(n * piece, piece), piece)
+            out = jnp.dot(act_s[...], wd_s[0, :, at], preferred_element_type=F32)
+            half_s[j, n, 0] = out[:half].astype(BF)
+            half_s[j, n, 1] = out[half:].astype(BF)
+            half_copy(j, n).start()
+            return carry
+
+        lax.fori_loop(0, CHUNKS, contract, 0)
+
+    def give_back(j):
+        for n in range(CHUNKS):
+            half_copy(j, n).wait_recv()
+            sum_s[n] = (half_s[j, n, pool].astype(F32) + half_r[j, n].astype(F32)).astype(BF)
+        for i in groups[j]:
+            k = i % planes * pairs
+            stacked = sum_s[:, k : k + pairs, :].reshape(tile, piece)
+            out = jnp.dot(perm_s[1], stacked, preferred_element_type=F32).astype(BF)
+            back_s[pl.ds(behind_y[i] * R, R)] = out.reshape(R, PAIR, piece)
+        for d in sent(j, -1):
+            back_copy(d, to(d), me).start()
+
+    collect(0)
+    apply(0)
+    collect(1)
+    give_back(0)
+    apply(1)
+    give_back(1)
     back_r[me] = back_s[me]
     for d in far:
         back_copy(d, me, source(d)).wait_recv()
@@ -337,9 +371,10 @@
         disp_copy(d, to(d), me).wait_send()
         back_copy(d, to(d), me).wait_send()
     for i in range(G):
-        rows_copy(i, pool, behind_y[i]).wait_send()
-    for n in range(CHUNKS):
-        half_copy(n).wait_send()
+        rows_copy(i, pool).wait_send()
+    for j in range(2):
+        for n in range(CHUNKS):
+            half_copy(j, n).wait_send()
 
 
 def per_device(
@@ -380,18 +415,20 @@
         pltpu.VMEM((E, few, block), F32),
         pltpu.VMEM((E * PAIR, CHUNKS * few), BF),
         pltpu.VMEM((2, CHUNKS * few, E * PAIR), BF),
+        pltpu.VMEM((2, R * PAIR, R * PAIR), BF),
         pltpu.VMEM((E, PAIR, piece), BF),
         pltpu.VMEM((E, PAIR, piece), BF),
-        pltpu.VMEM((2 * side, model), BF),
-        pltpu.VMEM((2 * side, hidden), BF),
-        pltpu.VMEM((CHUNKS, 2, side, piece), BF),
-        pltpu.VMEM((CHUNKS, side, piece), BF),
-        pltpu.VMEM((CHUNKS, side, piece), BF),
+        pltpu.VMEM((2, side, model), BF),
+        pltpu.VMEM((side, hidden), BF),
+        pltpu.VMEM((2, CHUNKS, 2, side // 2, piece), BF),
+        pltpu.VMEM((2, CHUNKS, side // 2, piece), BF),
+        pltpu.VMEM((CHUNKS, side // 2, piece), BF),
         pltpu.VMEM((E, PAIR, piece), BF),
         pltpu.VMEM((E, PAIR, piece), BF),
     ]
-    for count in (R - 1, R - 1, R - 1, E - 1, E - 1, G, CHUNKS, E - 1):
-        scratch += [dma((count,)), dma((count,))]
+    for count in (R - 1, R - 1, R - 1, E - 1, E - 1, G, (2, CHUNKS), E - 1):
+        shape = count if isinstance(count, tuple) else (count,)
+        scratch += [dma(shape), dma(shape)]
     return pl.pallas_call(
         functools.partial(layer, G, R),
         out_shape=[jax.ShapeDtypeStruct(hidden_in.shape, BF)] * 2,

time: 102 us -> 96.9 us (0.950)
  Pallas kernels: 97.7 us -> 93.1 us
    pallas_call x1, Pallas kernels: 97.7 us -> 93.1 us  [per_device(): pl.pallas_call(functools.partial(layer, G, R), out_shape=[jax.ShapeDtypeS...]
where the time goes in v4:
time: 96.9 us; the launch traced here: 96.5 us
  Pallas kernels  93.1 us (96%)
  local copies, waits for them, and re-layouts  2.77 us (3%)
    pallas_call x1, Pallas kernels, per_device(): pl.pallas_call(functools.partial(layer, G, R), out_shape=[jax.ShapeDtypeS...  93.1 us
    unnamed x2, local copies, waits for them, and re-layouts  2.77 us

profile of v4, /device:TPU:1, one launch (start us, length us, event | category | flops | bytes accessed | tf_op | source)
XLA Modules:
  0.0 96.5 jit_solution(3124250161188285268)
XLA Ops:
  0.6 93.1 %decode_layer.1 = (bf16[4,4096]{1,0:T(4,128)(2,1)}, bf16[4,4096]{1,0:T(4,128)(2,1)}) custom-call(bf16[256,2048]{1,0:T(8,128)(2,1)} %q_hbm.1, bf16[1024,128]{1,0:T(8,128)(2,1)} %k_hbm.1, bf16[1024,128]{1,0:T(8,128)(2,1)} %v_hbm.1, bf16[2048,256]{1,0:T(8,128)(2,1)} %ow_hbm.1, bf16[4,4096]{1,0:T(4,128)(2,1)} %hidden_ref.1, bf16[4096]{0:T(1024)(128)(2,1)} %gain_ref.1, ...), custom_call_target="tpu_custom_call" | custom-call | tf_op jit(solution)/shard_map/decode_layer/pallas_call | solution.py:432
  93.8 1.4 %copy.15 = bf16[4,4096]{1,0:T(4,128)(2,1)} copy(bf16[4,4096]{1,0:T(4,128)(2,1)} %get-tuple-element.4) | data formatting | bytes 65536
  95.2 1.4 %copy.16 = bf16[4,4096]{1,0:T(4,128)(2,1)} copy(bf16[4,4096]{1,0:T(4,128)(2,1)} %get-tuple-element.5) | data formatting | bytes 65536

commit v5 on v4

--- a/solution.py
+++ b/solution.py
@@ -33,10 +33,11 @@
     q_hbm, k_hbm, v_hbm, ow_hbm, hidden_ref, gain_ref, routes_ref, weights_ref, wg_hbm, wu_hbm, wd_hbm,
     mid_ref, mix_ref,
     q_s, k_s, v_s, ow_s, wg_s, wu_s, wd_s, load_sem,
-    part_s, stat_s, part_r, stat_r, attn_s,
+    known, part_s, stat_s, part_r, stat_r, next_s, tops_s, next_r, tops_r, attn_s,
     cols_s, cols_r, sel_s, comb_s, perm_s,
     disp_s, disp_r, rows_s, act_s, half_s, half_r, sum_s, back_s, back_r,
-    part_ss, part_rs, stat_ss, stat_rs, attn_ss, attn_rs,
+    part_ss, part_rs, stat_ss, stat_rs, next_ss, next_rs, tops_ss, tops_rs,
+    pass_ss, pass_rs, wide_ss, wide_rs,
     cols_ss, cols_rs, disp_ss, disp_rs,
     rows_ss, rows_rs, half_ss, half_rs, back_ss, back_rs,
 ):
@@ -63,7 +64,6 @@
         d, plane = d % R, d // R
         return behind_y[plane], behind_x[d // wide] + behind_z[d % wide]
 
-    near = [i * (R // 2 - 1) % R for i in range(1, R)]
     far = [i * (E // 2 - 5) % E for i in range(1, E)]
 
     loads = [
@@ -84,8 +84,16 @@
         load.start()
 
     barrier = pltpu.get_barrier_semaphore()
-    for d in far:
-        pl.semaphore_signal(barrier, inc=1, device_id=(pool, *ahead(d)), device_id_type=MESH)
+    along_x = [d * wide for d in range(1, wide)]
+    along_z = list(range(1, wide))
+    along_y = [d * R for d in range(1, G)]
+    axes = along_x + along_z + along_y
+
+    def greet(sem, shifts):
+        for d in shifts:
+            pl.semaphore_signal(sem, inc=1, device_id=(pool, *ahead(d)), device_id_type=MESH)
+
+    greet(barrier, axes)
     pl.semaphore_signal(barrier, inc=1, device_id=sibling, device_id_type=MESH)
 
     for load in loads[:3]:
@@ -93,89 +101,130 @@
     loads[3].start()
 
     rows_all, width = q_s.shape
-    heads = width // HEAD_DIM
+    heads = width // HEAD_DIM // 2
     share = rows_all // R
     lanes = share * heads
     scale = HEAD_DIM ** (-0.5)
-    order = R // 2 - 1
-
-    def target(s):
-        d = lax.rem((s + 1) * order, R)
-        across = lax.rem(x + way * (d // wide) + wide, wide)
-        return across * wide + lax.rem(z + way * lax.rem(d, wide) + wide, wide)
-
-    def part_copy(s, peer):
-        where = (pool, grp, peer)
-        return (
-            remote(part_s.at[s], part_r.at[s], part_ss.at[s], part_rs.at[s], where),
-            remote(stat_s.at[s], stat_r.at[s], stat_ss.at[s], stat_rs.at[s], where),
-        )
-
-    def attend(s):
-        peer = target(s)
-        block = pl.ds(pl.multiple_of(peer * share, share), share)
-        query = jnp.concatenate(
-            [q_s[block, h * HEAD_DIM : (h + 1) * HEAD_DIM] for h in range(heads)], axis=0
-        )
-        scores = lax.dot_general(
-            query, k_s[...], (((1,), (1,)), ((), ())), preferred_element_type=F32
-        )
-        top = jnp.max(scores, axis=1, keepdims=True)
-        probs = jnp.exp((scores - top) * scale)
-        total = jnp.sum(probs, axis=1, keepdims=True)
-        part = jnp.dot(probs.astype(BF), v_s[...], preferred_element_type=F32)
-        part_s[s] = part.astype(BF)
-        first = lax.broadcasted_iota(jnp.int32, (lanes, 128), 1) < 4
-        stat_s[s] = jnp.where(first, top, total).T[:8]
-
-    unroll = 4
-
-    def attend_some(i, carry):
-        for j in range(unroll):
-            s = i * unroll + j
-            attend(s)
-
-            @pl.when(s < R - 1)
-            def _():
-                for copy in part_copy(s, target(s)):
+    few, topk = routes_ref.shape
+    firsts, seconds = (along_x, along_z), (along_z, along_x)
+    across = ([x * wide for x in range(wide)], list(range(wide)))
+    orders = [*range(2, wide), 1, 0] if wide > 2 else [1, 0]
+    here = (x, z)
+
+    def part_copy(h, k):
+        where = (pool, *ahead(firsts[h][k - 1]))
+        return [
+            remote(a.at[h, k], b.at[h, k - 1], c.at[h, k - 1], d.at[h, k - 1], where)
+            for a, b, c, d in ((part_s, part_r, part_ss, part_rs), (stat_s, stat_r, stat_ss, stat_rs))
+        ]
+
+    def attend(h, k):
+        start = ahead_x[k] if h == 0 else ahead_z[k]
+        for pair in range(0, wide, 2):
+            pieces = []
+            for other in (pair, pair + 1):
+                row = pl.multiple_of((start + across[1 - h][other]) * share, share)
+                for head in range(h * heads, (h + 1) * heads):
+                    pieces.append(
+                        q_s[pl.ds(row, share), head * HEAD_DIM : (head + 1) * HEAD_DIM]
+                    )
+            query = jnp.concatenate(pieces, axis=0)
+            scores = lax.dot_general(
+                query, k_s[...], (((1,), (1,)), ((), ())), preferred_element_type=F32
+            )
+            top = jnp.max(scores, axis=1, keepdims=True)
+            probs = jnp.exp((scores - top) * scale)
+            total = jnp.sum(probs, axis=1, keepdims=True)
+            part = jnp.dot(probs.astype(BF), v_s[...], preferred_element_type=F32)
+            part_s[h, k, pair * lanes : (pair + 2) * lanes] = part.astype(BF)
+            first = lax.broadcasted_iota(jnp.int32, (2 * lanes, 128), 1) < 4
+            stat_s[h, k, :, pair * lanes : (pair + 2) * lanes] = (
+                jnp.where(first, top, total).T[:8]
+            )
+
+    met = False
+    for k in orders:
+        for h in range(2):
+            attend(h, k)
+            if not met:
+                pl.semaphore_wait(barrier, len(axes) + 1)
+                greet(known.at[0], along_x)
+                met = True
+            if k:
+                for copy in part_copy(h, k):
                     copy.start()
 
-        return carry
-
-    few, topk = routes_ref.shape
-    for s in range(unroll):
-        attend(s)
-    pl.semaphore_wait(barrier, E)
-    for s in range(min(unroll, R - 1)):
-        for copy in part_copy(s, target(s)):
-            copy.start()
-    lax.fori_loop(1, R // unroll, attend_some, 0)
-    for s in range(R - 1):
-        for copy in part_copy(s, rep):
-            copy.wait_recv()
-
-    stats = [stat_r[s] for s in range(R - 1)] + [stat_s[R - 1]]
-    top = functools.reduce(jnp.maximum, [stat[0:1] for stat in stats])
-    factors = [jnp.exp((stat[0:1] - top) * scale) for stat in stats]
-    total = functools.reduce(
-        jnp.add, [stat[4:5] * factor for stat, factor in zip(stats, factors)]
-    )
-    factors = [factor / total for factor in factors]
-    factors = jnp.concatenate(factors + [jnp.zeros((128 - R, lanes), F32)], axis=0).T
-    weighted = part_s[R - 1].astype(F32) * factors[:, R - 1 : R]
-    for s in range(R - 1):
-        weighted += part_r[s].astype(F32) * factors[:, s : s + 1]
-    attention = weighted.astype(BF)
-    mine = pl.ds(pl.multiple_of(rep * share, share), share)
-    for h in range(heads):
-        attn_s[mine, h * HEAD_DIM : (h + 1) * HEAD_DIM] = attention[h * share : (h + 1) * share]
-
-    def attn_copy(d, block):
-        at = attn_s.at[pl.ds(pl.multiple_of(block * share, share), share)]
-        return remote(at, at, attn_ss.at[d - 1], attn_rs.at[d - 1], (pool, *ahead(d)))
-
-    for d in near:
-        attn_copy(d, rep).start()
+    def merged(parts, stats, divide):
+        top = functools.reduce(jnp.maximum, [stat[0:1] for stat in stats])
+        factors = [jnp.exp((stat[0:1] - top) * scale) for stat in stats]
+        total = functools.reduce(
+            jnp.add, [stat[4:5] * factor for stat, factor in zip(stats, factors)]
+        )
+        if divide:
+            factors = [factor / total for factor in factors]
+        empty = jnp.zeros((128 - len(stats), top.shape[1]), F32)
+        columns = jnp.concatenate(factors + [empty], axis=0).T
+        out = functools.reduce(
+            jnp.add, [part.astype(F32) * columns[:, i : i + 1] for i, part in enumerate(parts)]
+        )
+        return out.astype(BF), top, total
+
+    def next_copy(h, k):
+        d = seconds[h][k - 1]
+        there = (ahead_z[k] if h == 0 else ahead_x[k] // wide)
+        where = (pool, *ahead(d))
+        return [
+            remote(a.at[h, there], b.at[h, k - 1], c.at[h, k - 1], d.at[h, k - 1], where)
+            for a, b, c, d in ((next_s, next_r, next_ss, next_rs), (tops_s, tops_r, tops_ss, tops_rs))
+        ]
+
+    for h in range(2):
+        for k in range(1, wide):
+            for copy in part_copy(h, k):
+                copy.wait_recv()
+        out, top, total = merged(
+            [part_s[h, 0]] + [part_r[h, k] for k in range(wide - 1)],
+            [stat_s[h, 0]] + [stat_r[h, k] for k in range(wide - 1)],
+            False,
+        )
+        first = lax.broadcasted_iota(jnp.int32, (8, lanes), 0) < 4
+        for other in range(wide):
+            at = slice(other * lanes, (other + 1) * lanes)
+            next_s[h, other] = out[at]
+            tops_s[h, other] = jnp.where(first, top[:, at], total[:, at])
+        for k in range(1, wide):
+            for copy in next_copy(h, k):
+                copy.start()
+    pl.semaphore_wait(known.at[0], wide - 1)
+    greet(known.at[1], along_y)
+
+    def pass_copy(h, k, block):
+        at = attn_s.at[h, here[h], block]
+        where = (pool, *ahead(seconds[h][k - 1]))
+        return remote(at, at, pass_ss.at[h, k - 1], pass_rs.at[h, k - 1], where)
+
+    def wide_copy(h, k, block):
+        at = attn_s.at[h, block]
+        where = (pool, *ahead(firsts[h][k - 1]))
+        return remote(at, at, wide_ss.at[h, k - 1], wide_rs.at[h, k - 1], where)
+
+    behind_of = (behind_z, [v // wide for v in behind_x])
+    for h in range(2):
+        for k in range(1, wide):
+            for copy in next_copy(h, k):
+                copy.wait_recv()
+        mine = here[1 - h]
+        out, _, _ = merged(
+            [next_s[h, mine]] + [next_r[h, k] for k in range(wide - 1)],
+            [tops_s[h, mine]] + [tops_r[h, k] for k in range(wide - 1)],
+            True,
+        )
+        for head in range(heads):
+            attn_s[h, here[h], mine, :, head * HEAD_DIM : (head + 1) * HEAD_DIM] = out[
+                head * share : (head + 1) * share
+            ]
+        for k in range(1, wide):
+            pass_copy(h, k, mine).start()
     for load in loads[4:]:
         load.start()
 
@@ -212,12 +261,30 @@
     perm_s[0] = jnp.where(col == moved(row), 1.0, 0.0).astype(BF)
     perm_s[1] = jnp.where(row == moved(col), 1.0, 0.0).astype(BF)
 
-    for d in near:
-        attn_copy(d, behind(d)[1]).wait_recv()
+    for h in range(2):
+        for k in range(1, wide):
+            pass_copy(h, k, behind_of[h][k]).wait_recv()
+        for k in range(1, wide):
+            wide_copy(h, k, here[h]).start()
+    for h in range(2):
+        for k in range(1, wide):
+            wide_copy(h, k, behind_of[1 - h][k]).wait_recv()
     loads[3].wait()
-    projected = jnp.dot(attn_s[...], ow_s[...], preferred_element_type=F32)
+    middle = width // 2
+    straight, turned = [
+        jnp.dot(
+            attn_s[h].reshape(rows_all, middle),
+            ow_s[h * middle : (h + 1) * middle, :],
+            preferred_element_type=F32,
+        )
+        for h in range(2)
+    ]
     for e in range(E):
-        cols_s[e] = projected[e * few : (e + 1) * few]
+        at = e * few
+        block = at // share
+        other = (block % wide * wide + block // wide) * share + at % share
+        cols_s[e] = straight[at : at + few] + turned[other : other + few]
+    pl.semaphore_wait(known.at[1], G - 1)
 
     def pair_copy(src, dst, send, recv, d, a, b):
         return remote(
@@ -361,11 +428,12 @@
     for c in range(CHUNKS):
         mix_ref[:, c * piece : (c + 1) * piece] = mixed[c * few : (c + 1) * few].astype(BF)
 
-    for s in range(R - 1):
-        for copy in part_copy(s, rep):
-            copy.wait_send()
-    for d in near:
-        attn_copy(d, rep).wait_send()
+    for h in range(2):
+        for k in range(1, wide):
+            for copy in part_copy(h, k) + next_copy(h, k):
+                copy.wait_send()
+            pass_copy(h, k, here[1 - h]).wait_send()
+            wide_copy(h, k, here[h]).wait_send()
     for d in far:
         cols_copy(d, to(d), me).wait_send()
         disp_copy(d, to(d), me).wait_send()
@@ -389,7 +457,8 @@
     hidden = w_gate.shape[2]
     heads = width // HEAD_DIM
     share = rows_all // R
-    lanes = share * heads
+    lanes = share * heads // 2
+    wide = math.isqrt(R)
     piece = model // CHUNKS
     side = E * SLOTS
 
@@ -406,11 +475,16 @@
         pltpu.VMEM(w_up.shape, BF),
         pltpu.VMEM(w_down.shape, BF),
         dma((7,)),
-        pltpu.VMEM((R, lanes, HEAD_DIM), BF),
-        pltpu.VMEM((R, 8, lanes), F32),
-        pltpu.VMEM((R - 1, lanes, HEAD_DIM), BF),
-        pltpu.VMEM((R - 1, 8, lanes), F32),
-        pltpu.VMEM((rows_all, width), BF),
+        pltpu.SemaphoreType.REGULAR((2,)),
+        pltpu.VMEM((2, wide, wide * lanes, HEAD_DIM), BF),
+        pltpu.VMEM((2, wide, 8, wide * lanes), F32),
+        pltpu.VMEM((2, wide - 1, wide * lanes, HEAD_DIM), BF),
+        pltpu.VMEM((2, wide - 1, 8, wide * lanes), F32),
+        pltpu.VMEM((2, wide, lanes, HEAD_DIM), BF),
+        pltpu.VMEM((2, wide, 8, lanes), F32),
+        pltpu.VMEM((2, wide - 1, lanes, HEAD_DIM), BF),
+        pltpu.VMEM((2, wide - 1, 8, lanes), F32),
+        pltpu.VMEM((2, wide, wide, share, width // 2), BF),
         pltpu.VMEM((E, few, block), F32),
         pltpu.VMEM((E, few, block), F32),
         pltpu.VMEM((E * PAIR, CHUNKS * few), BF),
@@ -426,7 +500,7 @@
         pltpu.VMEM((E, PAIR, piece), BF),
         pltpu.VMEM((E, PAIR, piece), BF),
     ]
-    for count in (R - 1, R - 1, R - 1, E - 1, E - 1, G, (2, CHUNKS), E - 1):
+    for count in [(2, wide - 1)] * 6 + [E - 1, E - 1, G, (2, CHUNKS), E - 1]:
         shape = count if isinstance(count, tuple) else (count,)
         scratch += [dma(shape), dma(shape)]
     return pl.pallas_call(

time: 96.9 us -> 90.3 us (0.932)
  Pallas kernels: 93.1 us -> 86.5 us
    pallas_call x1, Pallas kernels: 93.1 us -> 86.5 us  [per_device(): pl.pallas_call(functools.partial(layer, G, R), out_shape=[jax.ShapeDtypeS...]
where the time goes in v5:
time: 90.3 us; the launch traced here: 89.9 us
  Pallas kernels  86.5 us (96%)
  local copies, waits for them, and re-layouts  2.77 us (3%)
    pallas_call x1, Pallas kernels, per_device(): pl.pallas_call(functools.partial(layer, G, R), out_shape=[jax.ShapeDtypeS...  86.5 us
    unnamed x2, local copies, waits for them, and re-layouts  2.77 us

profile of v5, /device:TPU:1, one launch (start us, length us, event | category | flops | bytes accessed | tf_op | source)
XLA Modules:
  0.0 89.9 jit_solution(526359052968265584)
XLA Ops:
  0.6 86.5 %decode_layer.1 = (bf16[4,4096]{1,0:T(4,128)(2,1)}, bf16[4,4096]{1,0:T(4,128)(2,1)}) custom-call(bf16[256,2048]{1,0:T(8,128)(2,1)} %q_hbm.1, bf16[1024,128]{1,0:T(8,128)(2,1)} %k_hbm.1, bf16[1024,128]{1,0:T(8,128)(2,1)} %v_hbm.1, bf16[2048,256]{1,0:T(8,128)(2,1)} %ow_hbm.1, bf16[4,4096]{1,0:T(4,128)(2,1)} %hidden_ref.1, bf16[4096]{0:T(1024)(128)(2,1)} %gain_ref.1, ...), custom_call_target="tpu_custom_call" | custom-call | tf_op jit(solution)/shard_map/decode_layer/pallas_call | solution.py:506
  87.1 1.4 %copy.15 = bf16[4,4096]{1,0:T(4,128)(2,1)} copy(bf16[4,4096]{1,0:T(4,128)(2,1)} %get-tuple-element.4) | data formatting | bytes 65536
  88.5 1.4 %copy.16 = bf16[4,4096]{1,0:T(4,128)(2,1)} copy(bf16[4,4096]{1,0:T(4,128)(2,1)} %get-tuple-element.5) | data formatting | bytes 65536

commit v6 on v5

--- a/solution.py
+++ b/solution.py
@@ -31,14 +31,14 @@
 def layer(
     G, R,
     q_hbm, k_hbm, v_hbm, ow_hbm, hidden_ref, gain_ref, routes_ref, weights_ref, wg_hbm, wu_hbm, wd_hbm,
-    mid_ref, mix_ref,
+    out_ref,
     q_s, k_s, v_s, ow_s, wg_s, wu_s, wd_s, load_sem,
     known, part_s, stat_s, part_r, stat_r, next_s, tops_s, next_r, tops_r, attn_s,
-    cols_s, cols_r, sel_s, comb_s, perm_s,
+    proj_f, proj_s, proj_r, cols_s, cols_r, sel_s, comb_s, perm_s,
     disp_s, disp_r, rows_s, act_s, half_s, half_r, sum_s, back_s, back_r,
     part_ss, part_rs, stat_ss, stat_rs, next_ss, next_rs, tops_ss, tops_rs,
     pass_ss, pass_rs, wide_ss, wide_rs,
-    cols_ss, cols_rs, disp_ss, disp_rs,
+    proj_ss, proj_rs, cols_ss, cols_rs, disp_ss, disp_rs,
     rows_ss, rows_rs, half_ss, half_rs, back_ss, back_rs,
 ):
     pool, grp, rep = lax.axis_index("pool"), lax.axis_index("grp"), lax.axis_index("rep")
@@ -279,21 +279,40 @@
         )
         for h in range(2)
     ]
-    for e in range(E):
-        at = e * few
-        block = at // share
-        other = (block % wide * wide + block // wide) * share + at % share
-        cols_s[e] = straight[at : at + few] + turned[other : other + few]
-    pl.semaphore_wait(known.at[1], G - 1)
+    tall = rows_all // G
+    for g in range(G):
+        other = jnp.concatenate(
+            [
+                turned[(b % wide * wide + b // wide) * share :][:share]
+                for b in range(g * tall // share, (g + 1) * tall // share)
+            ],
+            axis=0,
+        )
+        proj_f[g] = straight[g * tall : (g + 1) * tall] + other
+        proj_s[g] = proj_f[g].astype(BF)
+
+    def proj_copy(d):
+        there = ahead_y[d]
+        return remote(
+            proj_s.at[there], proj_r.at[d - 1], proj_ss.at[d - 1], proj_rs.at[d - 1],
+            (pool, there, rep),
+        )
+
+    for d in range(1, G):
+        proj_copy(d).start()
+    summed = proj_f[grp]
+    for d in range(1, G):
+        proj_copy(d).wait_recv()
+        summed = summed + proj_r[d - 1].astype(F32)
+    summed = summed.astype(BF).astype(F32)
+    for j in range(R):
+        cols_s[j] = summed[j * few : (j + 1) * few]
 
     def pair_copy(src, dst, send, recv, d, a, b):
         return remote(
             src.at[a], dst.at[b], send.at[d - 1], recv.at[d - 1], (pool, *ahead(d))
         )
 
-    def cols_copy(d, a, b):
-        return pair_copy(cols_s, cols_r, cols_ss, cols_rs, d, a, b)
-
     def disp_copy(d, a, b):
         return pair_copy(disp_s, disp_r, disp_ss, disp_rs, d, a, b)
 
@@ -308,19 +327,21 @@
         there, along = behind(d)
         return there * R + along
 
-    for d in far:
-        cols_copy(d, to(d), me).start()
-    cols_r[me] = cols_s[me]
-    for d in far:
-        cols_copy(d, me, source(d)).wait_recv()
-    summed = cols_r[0:R]
-    for g in range(1, G):
-        summed = summed + cols_r[g * R : (g + 1) * R]
-    summed = summed.astype(BF).astype(F32)
-    projected = jnp.concatenate([summed[j] for j in range(R)], axis=1)
+    near = [i * (R // 2 - 1) % R for i in range(1, R)]
+
+    def cols_copy(d, a, b):
+        return pair_copy(cols_s, cols_r, cols_ss, cols_rs, d, a, b)
+
+    for d in near:
+        cols_copy(d, ahead(d)[1], rep).start()
+    cols_r[rep] = cols_s[rep]
+    for d in near:
+        cols_copy(d, rep, behind(d)[1]).wait_recv()
+    pl.semaphore_wait(known.at[1], G - 1)
+    projected = jnp.concatenate([cols_r[j] for j in range(R)], axis=1)
     mid = (hidden_ref[...].astype(F32) + projected).astype(BF)
-    mid_ref[...] = mid
     wider = mid.astype(F32)
+    out_ref[0] = mid
     inverse = lax.rsqrt(jnp.mean(wider * wider, axis=-1, keepdims=True) + 1e-06)
     normed = wider * inverse * gain_ref[...].astype(F32).reshape(1, -1)
     piece = normed.shape[1] // CHUNKS
@@ -426,7 +447,7 @@
         comb_s[1], returned, preferred_element_type=F32
     )
     for c in range(CHUNKS):
-        mix_ref[:, c * piece : (c + 1) * piece] = mixed[c * few : (c + 1) * few].astype(BF)
+        out_ref[1, :, c * piece : (c + 1) * piece] = mixed[c * few : (c + 1) * few].astype(BF)
 
     for h in range(2):
         for k in range(1, wide):
@@ -434,8 +455,11 @@
                 copy.wait_send()
             pass_copy(h, k, here[1 - h]).wait_send()
             wide_copy(h, k, here[h]).wait_send()
+    for d in range(1, G):
+        proj_copy(d).wait_send()
+    for d in near:
+        cols_copy(d, ahead(d)[1], rep).wait_send()
     for d in far:
-        cols_copy(d, to(d), me).wait_send()
         disp_copy(d, to(d), me).wait_send()
         back_copy(d, to(d), me).wait_send()
     for i in range(G):
@@ -459,6 +483,7 @@
     share = rows_all // R
     lanes = share * heads // 2
     wide = math.isqrt(R)
+    tall = rows_all // G
     piece = model // CHUNKS
     side = E * SLOTS
 
@@ -485,8 +510,11 @@
         pltpu.VMEM((2, wide - 1, lanes, HEAD_DIM), BF),
         pltpu.VMEM((2, wide - 1, 8, lanes), F32),
         pltpu.VMEM((2, wide, wide, share, width // 2), BF),
-        pltpu.VMEM((E, few, block), F32),
-        pltpu.VMEM((E, few, block), F32),
+        pltpu.VMEM((G, tall, block), F32),
+        pltpu.VMEM((G, tall, block), BF),
+        pltpu.VMEM((G - 1, tall, block), BF),
+        pltpu.VMEM((R, few, block), F32),
+        pltpu.VMEM((R, few, block), F32),
         pltpu.VMEM((E * PAIR, CHUNKS * few), BF),
         pltpu.VMEM((2, CHUNKS * few, E * PAIR), BF),
         pltpu.VMEM((2, R * PAIR, R * PAIR), BF),
@@ -500,14 +528,14 @@
         pltpu.VMEM((E, PAIR, piece), BF),
         pltpu.VMEM((E, PAIR, piece), BF),
     ]
-    for count in [(2, wide - 1)] * 6 + [E - 1, E - 1, G, (2, CHUNKS), E - 1]:
+    for count in [(2, wide - 1)] * 6 + [G - 1, R - 1, E - 1, G, (2, CHUNKS), E - 1]:
         shape = count if isinstance(count, tuple) else (count,)
         scratch += [dma(shape), dma(shape)]
-    return pl.pallas_call(
+    out = pl.pallas_call(
         functools.partial(layer, G, R),
-        out_shape=[jax.ShapeDtypeStruct(hidden_in.shape, BF)] * 2,
+        out_shape=jax.ShapeDtypeStruct((2, few, model), BF),
         in_specs=[anywhere] * 4 + [vmem] * 2 + [smem] * 2 + [anywhere] * 3,
-        out_specs=[vmem] * 2,
+        out_specs=vmem,
         scratch_shapes=scratch,
         compiler_params=pltpu.CompilerParams(
             collective_id=0, has_side_effects=True, vmem_limit_bytes=58 << 20
@@ -518,6 +546,7 @@
         hidden_in, norm_gain, routes, route_weights,
         w_gate, w_up, w_down,
     )
+    return out[0], out[1]
 
 
 def solution(mesh):

time: 90.3 us -> 89 us (0.986)
  local copies, waits for them, and re-layouts: 2.77 us -> 1.43 us
    unnamed x2 -> x0, local copies, waits for them, and re-layouts: 2.77 us -> none
    squeeze x0 -> x1, local copies, waits for them, and re-layouts: none -> 1.43 us  [per_device(): return (out[0], out[1])]
where the time goes in v6:
time: 89 us; the launch traced here: 88.7 us
  Pallas kernels  86.6 us (97%)
  local copies, waits for them, and re-layouts  1.43 us (2%)
    pallas_call x1, Pallas kernels, per_device(): pl.pallas_call(functools.partial(layer, G, R), out_shape=jax.ShapeDtypeSt...  86.6 us

profile of v6, /device:TPU:1, one launch (start us, length us, event | category | flops | bytes accessed | tf_op | source)
XLA Modules:
  0.0 88.7 jit_solution(17503906785574629781)
XLA Ops:
  0.6 86.6 %decode_layer.1 = bf16[2,4,4096]{2,1,0:T(4,128)(2,1)} custom-call(bf16[256,2048]{1,0:T(8,128)(2,1)} %q_hbm.1, bf16[1024,128]{1,0:T(8,128)(2,1)} %k_hbm.1, bf16[1024,128]{1,0:T(8,128)(2,1)} %v_hbm.1, bf16[2048,256]{1,0:T(8,128)(2,1)} %ow_hbm.1, bf16[4,4096]{1,0:T(4,128)(2,1)} %hidden_ref.1, bf16[4096]{0:T(1024)(128)(2,1)} %gain_ref.1, s32[4,8]{1,0:T(4,128)} %routes_ref.1, ...), custom_call_target="tpu_custom_call" | custom-call | tf_op jit(solution)/shard_map/decode_layer/pallas_call | solution.py:534
  87.3 1.4 %slice_bitcast_fusion = (bf16[4,4096]{1,0:T(4,128)(2,1)}, bf16[4,4096]{1,0:T(4,128)(2,1)}) fusion(bf16[2,4,4096]{2,1,0:T(4,128)(2,1)} %decode_layer.1), kind=kLoop, calls=%fused_computation | loop fusion | bytes 131072 | tf_op jit(solution)/shard_map/squeeze | solution.py:549

commit v7 on v6

--- a/solution.py
+++ b/solution.py
@@ -9,6 +9,7 @@
 from jax.sharding import PartitionSpec as P
 
 HEAD_DIM = 128
+LOG2E = 1.4426950408889634
 CHUNKS = 8
 SLOTS = 2
 PAIR = CHUNKS * SLOTS
@@ -32,7 +33,7 @@
     G, R,
     q_hbm, k_hbm, v_hbm, ow_hbm, hidden_ref, gain_ref, routes_ref, weights_ref, wg_hbm, wu_hbm, wd_hbm,
     out_ref,
-    q_s, k_s, v_s, ow_s, wg_s, wu_s, wd_s, load_sem,
+    q_s, k_s, v_s, value_s, ow_s, wg_s, wu_s, wd_s, load_sem,
     known, part_s, stat_s, part_r, stat_r, next_s, tops_s, next_r, tops_r, attn_s,
     proj_f, proj_s, proj_r, cols_s, cols_r, sel_s, comb_s, perm_s,
     disp_s, disp_r, rows_s, act_s, half_s, half_r, sum_s, back_s, back_r,
@@ -99,6 +100,8 @@
     for load in loads[:3]:
         load.wait()
     loads[3].start()
+    value_s[:, :HEAD_DIM] = v_s[...]
+    value_s[:, HEAD_DIM:] = jnp.ones_like(v_s)
 
     rows_all, width = q_s.shape
     heads = width // HEAD_DIM // 2
@@ -133,10 +136,10 @@
                 query, k_s[...], (((1,), (1,)), ((), ())), preferred_element_type=F32
             )
             top = jnp.max(scores, axis=1, keepdims=True)
-            probs = jnp.exp((scores - top) * scale)
-            total = jnp.sum(probs, axis=1, keepdims=True)
-            part = jnp.dot(probs.astype(BF), v_s[...], preferred_element_type=F32)
-            part_s[h, k, pair * lanes : (pair + 2) * lanes] = part.astype(BF)
+            probs = jnp.exp2((scores - top) * (scale * LOG2E)).astype(BF)
+            part = jnp.dot(probs, value_s[...], preferred_element_type=F32)
+            total = part[:, HEAD_DIM:]
+            part_s[h, k, pair * lanes : (pair + 2) * lanes] = part[:, :HEAD_DIM].astype(BF)
             first = lax.broadcasted_iota(jnp.int32, (2 * lanes, 128), 1) < 4
             stat_s[h, k, :, pair * lanes : (pair + 2) * lanes] = (
                 jnp.where(first, top, total).T[:8]
@@ -146,11 +149,12 @@
     for k in orders:
         for h in range(2):
             attend(h, k)
-            if not met:
-                pl.semaphore_wait(barrier, len(axes) + 1)
-                greet(known.at[0], along_x)
-                met = True
-            if k:
+        if not met:
+            pl.semaphore_wait(barrier, len(axes) + 1)
+            greet(known.at[0], along_x)
+            met = True
+        if k:
+            for h in range(2):
                 for copy in part_copy(h, k):
                     copy.start()
 
@@ -349,8 +353,9 @@
         [normed[:, c * piece : (c + 1) * piece] for c in range(CHUNKS)], axis=0
     ).astype(BF)
 
-    planes = G // 2
-    groups = [range(j * planes, (j + 1) * planes) for j in range(2)]
+    groups = [[i for i in range(G) if i != G // 2], [G // 2]]
+    half = [len(group) * pairs for group in groups]
+    base = [0, 2 * half[0]]
 
     def sent(j, sign):
         return [d for d in far if sign * (d // R) % G in groups[j]]
@@ -367,10 +372,13 @@
         for d in sent(j, 1):
             disp_copy(d, to(d), me).start()
     disp_r[me] = disp_s[me]
-    half = planes * pairs
+    def rows_at(i, of):
+        j = int(i not in groups[0])
+        first = base[j] + of * half[j] + groups[j].index(i) * pairs
+        return pl.ds(pl.multiple_of(first, pairs), pairs)
 
     def rows_copy(i, of):
-        at = rows_s.at[i // planes, pl.ds(of * half + i % planes * pairs, pairs)]
+        at = rows_s.at[rows_at(i, of)]
         return remote(at, at, rows_ss.at[i], rows_rs.at[i], sibling)
 
     def collect(j):
@@ -380,59 +388,75 @@
                     disp_copy(d, me, source(d)).wait_recv()
             arrived = disp_r[pl.ds(behind_y[i] * R, R)].reshape(tile, piece)
             ordered = jnp.dot(perm_s[0], arrived, preferred_element_type=F32).astype(BF)
-            at = pl.ds(pl.multiple_of(pool * half + i % planes * pairs, pairs), pairs)
+            at = rows_at(i, pool)
             for c in range(CHUNKS):
-                rows_s[j, at, c * piece : (c + 1) * piece] = ordered[c * pairs : (c + 1) * pairs]
+                rows_s[at, c * piece : (c + 1) * piece] = ordered[c * pairs : (c + 1) * pairs]
             rows_copy(i, pool).start()
 
     hidden = act_s.shape[1]
     step = min(256, hidden)
 
     def half_copy(j, n):
+        at = pl.ds(0, half[j])
         return remote(
-            half_s.at[j, n, 1 - pool], half_r.at[j, n], half_ss.at[j, n], half_rs.at[j, n], sibling
+            half_s.at[j, n, 1 - pool, at], half_r.at[j, n, at],
+            half_ss.at[j, n], half_rs.at[j, n], sibling,
         )
 
     def apply(j):
         for i in groups[j]:
             rows_copy(i, 1 - pool).wait_recv()
+        mine = slice(base[j], base[j] + 2 * half[j])
+        both = slice(0, 2 * half[j])
         if j == 0:
             loads[4].wait()
             loads[5].wait()
 
         def expand(n, carry):
             at = pl.ds(pl.multiple_of(n * step, step), step)
-            gate = jnp.dot(rows_s[j], wg_s[0, :, at], preferred_element_type=F32)
-            upper = jnp.dot(rows_s[j], wu_s[0, :, at], preferred_element_type=F32)
-            act_s[:, at] = (gate / (1.0 + jnp.exp(-gate)) * upper).astype(BF)
+            gate = jnp.dot(rows_s[mine], wg_s[0, :, at], preferred_element_type=F32)
+            upper = jnp.dot(rows_s[mine], wu_s[0, :, at], preferred_element_type=F32)
+            act_s[both, at] = (gate / (1.0 + jnp.exp(-gate)) * upper).astype(BF)
             return carry
 
-        lax.fori_loop(0, hidden // step, expand, 0)
+        lax.fori_loop(0, hidden // step, expand, 0, unroll=True)
         if j == 0:
             loads[6].wait()
 
         def contract(n, carry):
             at = pl.ds(pl.multiple_of(n * piece, piece), piece)
-            out = jnp.dot(act_s[...], wd_s[0, :, at], preferred_element_type=F32)
-            half_s[j, n, 0] = out[:half].astype(BF)
-            half_s[j, n, 1] = out[half:].astype(BF)
+            out = jnp.dot(act_s[both], wd_s[0, :, at], preferred_element_type=F32)
+            half_s[j, n, 0, : half[j]] = out[: half[j]].astype(BF)
+            half_s[j, n, 1, : half[j]] = out[half[j] :].astype(BF)
             half_copy(j, n).start()
             return carry
 
-        lax.fori_loop(0, CHUNKS, contract, 0)
+        lax.fori_loop(0, CHUNKS, contract, 0, unroll=4)
 
     def give_back(j):
         for n in range(CHUNKS):
             half_copy(j, n).wait_recv()
-            sum_s[n] = (half_s[j, n, pool].astype(F32) + half_r[j, n].astype(F32)).astype(BF)
+            sum_s[n, : half[j]] = (
+                half_s[j, n, pool, : half[j]].astype(F32) + half_r[j, n, : half[j]].astype(F32)
+            ).astype(BF)
         for i in groups[j]:
-            k = i % planes * pairs
+            k = groups[j].index(i) * pairs
             stacked = sum_s[:, k : k + pairs, :].reshape(tile, piece)
             out = jnp.dot(perm_s[1], stacked, preferred_element_type=F32).astype(BF)
             back_s[pl.ds(behind_y[i] * R, R)] = out.reshape(R, PAIR, piece)
         for d in sent(j, -1):
             back_copy(d, to(d), me).start()
 
+    for h in range(2):
+        for k in range(1, wide):
+            for copy in part_copy(h, k) + next_copy(h, k):
+                copy.wait_send()
+            pass_copy(h, k, here[1 - h]).wait_send()
+            wide_copy(h, k, here[h]).wait_send()
+    for d in range(1, G):
+        proj_copy(d).wait_send()
+    for d in near:
+        cols_copy(d, ahead(d)[1], rep).wait_send()
     collect(0)
     apply(0)
     collect(1)
@@ -441,6 +465,14 @@
     give_back(1)
     back_r[me] = back_s[me]
     for d in far:
+        disp_copy(d, to(d), me).wait_send()
+        back_copy(d, to(d), me).wait_send()
+    for i in range(G):
+        rows_copy(i, pool).wait_send()
+    for j in range(2):
+        for n in range(CHUNKS):
+            half_copy(j, n).wait_send()
+    for d in far:
         back_copy(d, me, source(d)).wait_recv()
     returned = back_r[...].reshape(E * PAIR, piece)
     mixed = jnp.dot(comb_s[0], returned, preferred_element_type=F32) + jnp.dot(
@@ -448,25 +480,6 @@
     )
     for c in range(CHUNKS):
         out_ref[1, :, c * piece : (c + 1) * piece] = mixed[c * few : (c + 1) * few].astype(BF)
-
-    for h in range(2):
-        for k in range(1, wide):
-            for copy in part_copy(h, k) + next_copy(h, k):
-                copy.wait_send()
-            pass_copy(h, k, here[1 - h]).wait_send()
-            wide_copy(h, k, here[h]).wait_send()
-    for d in range(1, G):
-        proj_copy(d).wait_send()
-    for d in near:
-        cols_copy(d, ahead(d)[1], rep).wait_send()
-    for d in far:
-        disp_copy(d, to(d), me).wait_send()
-        back_copy(d, to(d), me).wait_send()
-    for i in range(G):
-        rows_copy(i, pool).wait_send()
-    for j in range(2):
-        for n in range(CHUNKS):
-            half_copy(j, n).wait_send()
 
 
 def per_device(
@@ -495,6 +508,7 @@
         pltpu.VMEM(queries.shape, BF),
         pltpu.VMEM(keys.shape, BF),
         pltpu.VMEM(values.shape, BF),
+        pltpu.VMEM((values.shape[0], 2 * HEAD_DIM), BF),
         pltpu.VMEM(o_weight.shape, BF),
         pltpu.VMEM(w_gate.shape, BF),
         pltpu.VMEM(w_up.shape, BF),
@@ -520,11 +534,11 @@
         pltpu.VMEM((2, R * PAIR, R * PAIR), BF),
         pltpu.VMEM((E, PAIR, piece), BF),
         pltpu.VMEM((E, PAIR, piece), BF),
-        pltpu.VMEM((2, side, model), BF),
-        pltpu.VMEM((side, hidden), BF),
-        pltpu.VMEM((2, CHUNKS, 2, side // 2, piece), BF),
-        pltpu.VMEM((2, CHUNKS, side // 2, piece), BF),
-        pltpu.VMEM((CHUNKS, side // 2, piece), BF),
+        pltpu.VMEM((2 * side, model), BF),
+        pltpu.VMEM((2 * side, hidden), BF),
+        pltpu.VMEM((2, CHUNKS, 2, side, piece), BF),
+        pltpu.VMEM((2, CHUNKS, side, piece), BF),
+        pltpu.VMEM((CHUNKS, side, piece), BF),
         pltpu.VMEM((E, PAIR, piece), BF),
         pltpu.VMEM((E, PAIR, piece), BF),
     ]

time: 89 us -> 87.5 us (0.983)
  Pallas kernels: 86.6 us -> 85.2 us
    pallas_call x1, Pallas kernels: 86.6 us -> 85.2 us  [per_device(): pl.pallas_call(functools.partial(layer, G, R), out_shape=jax.ShapeDtypeSt...]
where the time goes in v7:
time: 87.5 us; the launch traced here: 87.3 us
  Pallas kernels  85.2 us (97%)
  local copies, waits for them, and re-layouts  1.43 us (2%)
    pallas_call x1, Pallas kernels, per_device(): pl.pallas_call(functools.partial(layer, G, R), out_shape=jax.ShapeDtypeSt...  85.2 us

profile of v7, /device:TPU:1, one launch (start us, length us, event | category | flops | bytes accessed | tf_op | source)
XLA Modules:
  0.0 87.3 jit_solution(7432617372402010945)
XLA Ops:
  0.6 85.2 %decode_layer.1 = bf16[2,4,4096]{2,1,0:T(4,128)(2,1)} custom-call(bf16[256,2048]{1,0:T(8,128)(2,1)} %q_hbm.1, bf16[1024,128]{1,0:T(8,128)(2,1)} %k_hbm.1, bf16[1024,128]{1,0:T(8,128)(2,1)} %v_hbm.1, bf16[2048,256]{1,0:T(8,128)(2,1)} %ow_hbm.1, bf16[4,4096]{1,0:T(4,128)(2,1)} %hidden_ref.1, bf16[4096]{0:T(1024)(128)(2,1)} %gain_ref.1, s32[4,8]{1,0:T(4,128)} %routes_ref.1, ...), custom_call_target="tpu_custom_call" | custom-call | tf_op jit(solution)/shard_map/decode_layer/pallas_call | solution.py:548
  85.8 1.4 %slice_bitcast_fusion = (bf16[4,4096]{1,0:T(4,128)(2,1)}, bf16[4,4096]{1,0:T(4,128)(2,1)}) fusion(bf16[2,4,4096]{2,1,0:T(4,128)(2,1)} %decode_layer.1), kind=kLoop, calls=%fused_computation | loop fusion | bytes 131072 | tf_op jit(solution)/shard_map/squeeze | solution.py:563
